TPU v7x, 512 devices: a whole 4x8x8 slice. The times are simulated.
512 devices in a mesh: grp: 64 (over z, y), row: 8 (over x, core).
Axes of the slice: x: 4, y: 8, z: 8, core: 2. Of those that a mesh axis runs over, the one named last changes fastest.
Arguments:
- latents: bfloat16 [64, 16384], P('grp'), may hold values from -6 to 6
- frames: int32 [64], replicated, may hold values from 1 to 4, as said below
- offsets: int32 [64], replicated, may hold values from 0 to 1008, as said below
- assign: int32 [64], replicated, may hold values from 0 to 63, each once
- w_in: bfloat16 [16, 27, 384], replicated, may hold values from -0.3125 to 0.3125
- w_mid: bfloat16 [384, 27, 192], P('grp'), may hold values from -0.0625 to 0.0625
- w_out: bfloat16 [192, 27, 96], P('grp'), may hold values from -0.078125 to 0.078125
- gain_in: float32 [384], replicated, may hold values from 0.25 to 1.75
- gain_mid: float32 [192], replicated, may hold values from 0.25 to 1.75
- gain_out: float32 [96], replicated, may hold values from 0.25 to 1.75
Outputs:
- decoded: bfloat16 [64, 4, 64, 6144], P('grp', None, 'row')
Inputs may be any that keep to these rules, and one draw needn't show every extreme that they name: Some request has exactly 4 frames. The blocks of different requests do not intersect, and offsets[r] + 16 <= 1024 for every request; some request starts at 1008. `assign`: every request is decoded by exactly one group.
All inputs are finite; a program needn't handle non-finite values.
Results may differ from a plain program's by a relative error of at most 0.006.
Values may be sent and summed in bfloat16 or wider, within the bound.
A program may use at most 128 MiB of HBM per device.

v0:
```python
import jax
import jax.numpy as jnp
from jax import lax
from jax.sharding import PartitionSpec as P

RL = 2
WL = 16
FMAX = 4


def extended_2(cells, sides, width):
    for axis, dim in sides:
        count = lax.axis_size(axis)
        ends = count - 1
        head = lax.slice_in_dim(cells, 0, width, axis=dim)
        tail = lax.slice_in_dim(cells, cells.shape[dim] - width, cells.shape[dim], axis=dim)
        cells = jnp.concatenate(
            [
                lax.ppermute(tail, axis, [(i, (i + 1) % count) for i in range(ends)]),
                cells,
                lax.ppermute(head, axis, [((i + 1) % count, i) for i in range(ends)]),
            ],
            axis=dim,
        )
    return cells


def rms_silu(hidden, gain):
    mean_sq = jnp.mean(hidden * hidden, axis=-1, keepdims=True)
    scaled = hidden * lax.rsqrt(mean_sq + 1e-06) * gain
    return jax.nn.silu(scaled)


def causal_conv(extended, weight):
    count_t = extended.shape[0]
    count_r = extended.shape[1] - 2
    count_c = extended.shape[2]
    width_in = extended.shape[3]
    width_out = weight.shape[2]
    padded = jnp.pad(extended, ((2, 0), (0, 0), (1, 1), (0, 0)))
    total = jnp.zeros((count_t * count_r * count_c, width_out), jnp.float32)
    for time_tap in range(3):
        for row_tap in range(3):
            for col_tap in range(3):
                window = padded[
                    time_tap : time_tap + count_t,
                    row_tap : row_tap + count_r,
                    col_tap : col_tap + count_c,
                ]
                window = window.reshape(count_t * count_r * count_c, width_in)
                tap_index = 9 * time_tap + 3 * row_tap + col_tap
                total = total + jnp.dot(
                    window, weight[:, tap_index, :], preferred_element_type=jnp.float32
                )
    return total.reshape(count_t, count_r, count_c, width_out)


def upsample(values):
    return jnp.repeat(jnp.repeat(values, 2, axis=1), 2, axis=2)


def per_device(latents, frames, offsets, assign, w_in, w_mid, w_out, gain_in, gain_mid, gain_out):
    groups = lax.axis_size("grp")
    row_count = lax.axis_size("row")
    row_index = lax.axis_index("row")
    group_index = lax.axis_index("grp")
    channels = w_in.shape[0]
    cap_vals = latents.shape[1] // groups
    cap_tokens = cap_vals // channels
    span_len = cap_tokens // FMAX
    flat = latents[0]
    slot_ids = jnp.arange(cap_vals, dtype=jnp.int32)

    def select_span(request):
        start = offsets[request] * channels
        block = lax.dynamic_slice_in_dim(flat, start, cap_vals)
        keep = slot_ids < frames[request] * span_len * channels
        return jnp.where(keep, block, jnp.zeros((), block.dtype))

    outgoing = jax.vmap(select_span)(assign)
    incoming = lax.all_to_all(outgoing, "grp", split_axis=0, concat_axis=0, tiled=True)
    table = incoming.reshape(groups * cap_tokens, channels)
    request = assign[group_index]
    count = frames[request]
    fill_len = count * span_len
    image_rows = RL * row_count
    frame_ids = jnp.arange(FMAX, dtype=jnp.int32)[:, None, None]
    row_ids = row_index * RL + jnp.arange(RL, dtype=jnp.int32)[None, :, None]
    col_ids = jnp.arange(WL, dtype=jnp.int32)[None, None, :]
    position = (frame_ids * image_rows + row_ids) * WL + col_ids
    shard = jnp.minimum(position // fill_len, groups - 1)
    within = position % fill_len
    tokens = table[shard * cap_tokens + within]
    valid = (frame_ids < count)[..., None]
    latent_in = jnp.where(valid, tokens, jnp.zeros((), tokens.dtype))
    full_mid, full_out = (
        lax.all_gather(w_mid, "grp", axis=0, tiled=True),
        lax.all_gather(w_out, "grp", axis=0, tiled=True),
    )
    latent_ext = extended_2(latent_in, (("row", 1),), 1)
    act_in = rms_silu(causal_conv(latent_ext, w_in), gain_in).astype(jnp.bfloat16)
    mid_ext = extended_2(upsample(act_in), (("row", 1),), 1)
    act_mid = rms_silu(causal_conv(mid_ext, full_mid), gain_mid).astype(jnp.bfloat16)
    out_ext = extended_2(upsample(act_mid), (("row", 1),), 1)
    final = rms_silu(causal_conv(out_ext, full_out), gain_out)
    final = jnp.where(valid, final, jnp.zeros((), jnp.float32)).astype(jnp.bfloat16)
    return final.reshape(1, FMAX, 4 * RL, 4 * WL * final.shape[3])


def solution(mesh):
    placed = (
        P("grp", None),
        P(),
        P(),
        P(),
        P(),
        P("grp", None, None),
        P("grp", None, None),
        P(),
        P(),
        P(),
    )
    return jax.shard_map(
        per_device,
        mesh=mesh,
        in_specs=placed,
        out_specs=P("grp", None, "row", None),
        check_vma=False,
    )
```

profile of v0, /device:TPU:1, one launch (start us, length us, event | category | flops | bytes accessed | tf_op | source)
XLA Modules:
  0.0 352.4 jit_solution(12229377863620362657)
XLA Ops:
  8.7 1.4 gather_fusion
  11.2 94.7 %while.1 = (s32[]{:T(128)}, bf16[16384]{0:T(1024)(128)(2,1)S(1)}, s32[64,1]{0,1:T(1,128)S(1)}, bf16[64,256]{1,0:T(8,128)(2,1)S(1)}, s32[]{:T(128)}, /*index=5*/s32[]{:T(128)}) while((s32[]{:T(128)}, bf16[16384]{0:T(1024)(128)(2,1)S(1)}, s32[64,1]{0,1:T(1,128)S(1)}, bf16[64,256]{1,0:T(8,128)(2,1)S(1)}, s32[]{:T(128)}, /*index=5*/s32[]{:T(128)}) %tuple.141), condition=%wide.while_cond, body=%wide.while_body.sunk | while | flops 2 | bytes 3169 | solution.py:76
  107.8 17.2 %all-to-all-start = ((bf16[64,2,128]{2,1,0:T(2,128)(2,1)}), bf16[64,2,128]{2,1,0:T(2,128)(2,1)S(1)}, u32[]{:S(2)}, u32[]{:S(2)}) async-start(bf16[64,2,128]{2,1,0:T(2,128)(2,1)} %reshape.702), calls=%async_computation | async-start | bytes 65536 | tf_op jit(solution)/shard_map/all_to_all | solution.py:81
  125.1 1.3 dynamic_slice.6
  128.5 1.3 dynamic_slice.7
  131.8 4.0 %all-to-all-done = bf16[64,2,128]{2,1,0:T(2,128)(2,1)S(1)} async-done(((bf16[64,2,128]{2,1,0:T(2,128)(2,1)}), bf16[64,2,128]{2,1,0:T(2,128)(2,1)S(1)}, u32[]{:S(2)}, u32[]{:S(2)}) %all-to-all-start) | async-done | bytes 32800 | tf_op jit(solution)/shard_map/all_to_all | solution.py:81
  137.1 5.1 %collective-permute-start = (bf16[4,1,16,16]{3,2,1,0:T(8,128)(2,1)S(1)}, bf16[4,1,16,16]{3,2,1,0:T(8,128)(2,1)S(1)}, u32[]{:S(2)}, u32[]{:S(2)}) collective-permute-start(bf16[4,1,16,16]{3,2,1,0:T(8,128)(2,1)S(1)} %get-tuple-element.157), channel_id=1, source_target_pairs={{0,1},{1,2},{2,3},{3,4},{4,5},{5,6},{6,7},{8,9},{9,10},{10,11},{11... | collective-permute-start | bytes 6152 | tf_op jit(solution)/shard_map/ppermute | solution.py:19
  142.2 1.9 collective-permute-start.1
  144.2 37.3 %all_gather.7 = bf16[192,27,96]{2,1,0:T(8,128)(2,1)S(1)} all-gather(bf16[3,27,96]{2,1,0:T(8,128)(2,1)S(1)} %copy-done.91), channel_id=1, replica_groups=mesh['grp'=64,'row'=8] {'grp'}, dimensions={0}, use_global_device_ids=true | all-gather | bytes 1010880 | tf_op jit(solution)/shard_map/all_gather | solution.py:98
  186.6 14.6 %collective-permute-start.2 = (bf16[4,1,32,384]{3,2,1,0:T(8,128)(2,1)S(1)}, bf16[4,1,32,384]{3,2,1,0:T(8,128)(2,1)S(1)}, u32[]{:S(2)}, u32[]{:S(2)}) collective-permute-start(bf16[4,1,32,384]{3,2,1,0:T(8,128)(2,1)S(1)} %get-tuple-element.129), channel_id=1, source_target_pairs={{0,1},{1,2},{2,3},{3,4},{4,5},{5,6},{6,7},{8,9},{9,10},{10,11},{11... | collective-permute-start | bytes 294920 | tf_op jit(solution)/shard_map/ppermute | solution.py:19
  201.2 2.4 collective-permute-start.3
  203.6 2.8 fusion.132
  208.7 1.4 fusion.135
  210.1 3.3 fusion.134
  213.5 8.5 %fusion.129 = (bf16[384,1,192]{2,1,0:T(2,128)(2,1)}, bf16[384,1,192]{2,1,0:T(2,128)(2,1)}, bf16[384,1,192]{2,1,0:T(2,128)(2,1)}, bf16[384,1,192]{2,1,0:T(2,128)(...) fusion(bf16[384,27,192]{2,1,0:T(8,128)(2,1)} %all-gather.2.clon, ...), kind=kLoop, calls=%fused_computation.270 | loop fusion | bytes 2359296 | tf_op jit(solution)/shard_map/slice | solution.py:53
  222.0 1.8 copy.135
  223.8 1.8 copy.134
  225.6 1.8 copy.133
  227.4 1.2 copy.132
  233.2 16.4 %fusion.128 = (bf16[384,1,192]{2,1,0:T(2,128)(2,1)}, bf16[384,1,192]{2,1,0:T(2,128)(2,1)}, bf16[384,1,192]{2,1,0:T(2,128)(2,1)}, bf16[384,1,192]{2,1,0:T(2,128)(...) fusion(bf16[384,27,192]{2,1,0:T(8,128)(2,1)} %all-gather.2.clon, ...), kind=kLoop, calls=%fused_computation.269 | loop fusion | bytes 5603328 | tf_op jit(solution)/shard_map/slice | solution.py:53
  249.6 1.8 copy.154
  251.4 1.8 copy.153
  253.2 1.8 copy.152
  255.0 1.8 copy.151
  256.8 1.8 copy.150
  258.6 1.8 copy.149
  260.4 1.8 copy.148
  262.2 1.8 copy.147
  264.0 1.8 copy.146
  265.8 1.8 copy.145
  268.7 1.8 copy.143
  271.7 1.2 copy.141
  272.9 1.8 copy.140
  274.7 1.8 copy.139
  276.5 1.8 copy.138
  279.4 1.3 copy.136
  280.8 1.3 fusion.64
  282.1 1.3 fusion.36
  283.4 1.2 fusion.43
  293.7 1.8 broadcast_in_dim.66
  295.5 2.1 reshape.625
  298.3 3.6 %collective-permute-start.4 = (bf16[4,1,64,192]{3,2,1,0:T(8,128)(2,1)}, bf16[4,1,64,192]{3,2,1,0:T(8,128)(2,1)S(1)}, u32[]{:S(2)}, u32[]{:S(2)}) collective-permute-start(bf16[4,1,64,192]{3,2,1,0:T(8,128)(2,1)} %get-tuple-element.125), channel_id=1, source_target_pairs={{0,1},{1,2},{2,3},{3,4},{4,5},{5,6},{6,7},{8,9},{9,10},{10,11},{11... | collective-permute-start | bytes 294920 | tf_op jit(solution)/shard_map/ppermute | solution.py:19
  301.9 1.9 collective-permute-start.5
  303.9 1.3 fusion.133
  305.2 2.9 reshape.648
  308.4 2.0 fusion.9
  310.5 3.1 fusion.131
  313.5 7.9 %fusion.130 = (bf16[4,8,64,192]{3,2,1,0:T(8,128)(2,1)S(1)}, bf16[4,8,64,192]{3,2,1,0:T(8,128)(2,1)S(1)}, bf16[4,8,64,192]{3,2,1,0:T(8,128)(2,1)S(1)}, bf16[4,8,6...) fusion(bf16[6,10,66,192]{3,2,1,0:T(8,128)(2,1)S(1)} %fusion.9), kind=kLoop, calls=%fused_computation.271 | loop fusion | bytes 29884416 | tf_op jit(solution)/shard_map/slice | solution.py:45
  (594 shorter events, 150.1 us)
Async XLA Ops:
  6.5 1.4 copy-start
  6.5 137.6 %copy-start.91 = (bf16[3,27,96]{2,1,0:T(8,128)(2,1)S(1)}, bf16[3,27,96]{2,1,0:T(8,128)(2,1)}, u32[]{:S(2)}) copy-start(bf16[3,27,96]{2,1,0:T(8,128)(2,1)} %param.16) | copy-start | bytes 46660
  6.5 206.9 %all-gather.2.cloned.1.call-start = ((), (), s32[]{:S(2)}) async-start(), calls=%async_computation.1 | async-start | bytes 6389760 | tf_op jit(solution)/shard_map/all_gather | solution.py:97
  107.8 73.9 %copy-start.69 = (bf16[16,27,384]{2,0,1:T(8,128)(2,1)S(1)}, bf16[16,27,384]{2,0,1:T(8,128)(2,1)}, u32[]{:S(2)}) copy-start(bf16[16,27,384]{2,0,1:T(8,128)(2,1)} %param.14) | copy-start | bytes 995332
  107.8 28.1 %all-to-all-start = ((bf16[64,2,128]{2,1,0:T(2,128)(2,1)}), bf16[64,2,128]{2,1,0:T(2,128)(2,1)S(1)}, u32[]{:S(2)}, u32[]{:S(2)}) async-start(bf16[64,2,128]{2,1,0:T(2,128)(2,1)} %reshape.702), calls=%async_computation | async-start | bytes 65536 | tf_op jit(solution)/shard_map/all_to_all | solution.py:81
  137.1 44.4 %collective-permute-start = (bf16[4,1,16,16]{3,2,1,0:T(8,128)(2,1)S(1)}, bf16[4,1,16,16]{3,2,1,0:T(8,128)(2,1)S(1)}, u32[]{:S(2)}, u32[]{:S(2)}) collective-permute-start(bf16[4,1,16,16]{3,2,1,0:T(8,128)(2,1)S(1)} %get-tuple-element.157), channel_id=1, source_target_pairs={{0,1},{1,2},{2,3},{3,4},{4,5},{5,6},{6,7},{8,9},{9,10},{10,11},{11... | collective-permute-start | bytes 6152 | tf_op jit(solution)/shard_map/ppermute | solution.py:19
  142.2 39.3 %collective-permute-start.1 = (bf16[4,1,16,16]{3,2,1,0:T(8,128)(2,1)S(1)}, bf16[4,1,16,16]{3,2,1,0:T(8,128)(2,1)S(1)}, u32[]{:S(2)}, u32[]{:S(2)}) collective-permute-start(bf16[4,1,16,16]{3,2,1,0:T(8,128)(2,1)S(1)} %get-tuple-element.158), channel_id=1, source_target_pairs={{1,0},{2,1},{3,2},{4,3},{5,4},{6,5},{7,6},{9,8},{10,9},{11,10},{12... | collective-permute-start | bytes 6152 | tf_op jit(solution)/shard_map/ppermute | solution.py:21
  184.4 1.6 copy-start.92
  186.6 20.8 %collective-permute-start.2 = (bf16[4,1,32,384]{3,2,1,0:T(8,128)(2,1)S(1)}, bf16[4,1,32,384]{3,2,1,0:T(8,128)(2,1)S(1)}, u32[]{:S(2)}, u32[]{:S(2)}) collective-permute-start(bf16[4,1,32,384]{3,2,1,0:T(8,128)(2,1)S(1)} %get-tuple-element.129), channel_id=1, source_target_pairs={{0,1},{1,2},{2,3},{3,4},{4,5},{5,6},{6,7},{8,9},{9,10},{10,11},{11... | collective-permute-start | bytes 294920 | tf_op jit(solution)/shard_map/ppermute | solution.py:19
  201.2 6.2 %collective-permute-start.3 = (bf16[4,1,32,384]{3,2,1,0:T(8,128)(2,1)S(1)}, bf16[4,1,32,384]{3,2,1,0:T(8,128)(2,1)S(1)}, u32[]{:S(2)}, u32[]{:S(2)}) collective-permute-start(bf16[4,1,32,384]{3,2,1,0:T(8,128)(2,1)S(1)} %get-tuple-element.130), channel_id=1, source_target_pairs={{1,0},{2,1},{3,2},{4,3},{5,4},{6,5},{7,6},{9,8},{10,9},{11,10},{12... | collective-permute-start | bytes 294920 | tf_op jit(solution)/shard_map/ppermute | solution.py:21
  268.7 12.1 %copy-start.22 = (bf16[4,4,32,384]{3,2,1,0:T(8,128)(2,1)S(1)}, bf16[4,4,32,384]{3,2,1,0:T(8,128)(2,1)}, u32[]{:S(2)}) copy-start(bf16[4,4,32,384]{3,2,1,0:T(8,128)(2,1)} %get-tuple-element.121) | copy-start | bytes 1179652
  271.7 10.3 %copy-start.21 = (bf16[4,4,32,384]{3,2,1,0:T(8,128)(2,1)S(1)}, bf16[4,4,32,384]{3,2,1,0:T(8,128)(2,1)}, u32[]{:S(2)}) copy-start(bf16[4,4,32,384]{3,2,1,0:T(8,128)(2,1)} %get-tuple-element.122) | copy-start | bytes 1179652
  272.9 10.5 %copy-start.23 = (bf16[4,4,32,384]{3,2,1,0:T(8,128)(2,1)S(1)}, bf16[4,4,32,384]{3,2,1,0:T(8,128)(2,1)}, u32[]{:S(2)}) copy-start(bf16[4,4,32,384]{3,2,1,0:T(8,128)(2,1)} %get-tuple-element.102) | copy-start | bytes 1179652
  279.4 5.5 %copy-start.43 = (bf16[4,4,32,384]{3,2,1,0:T(8,128)(2,1)S(1)}, bf16[4,4,32,384]{3,2,1,0:T(8,128)(2,1)}, u32[]{:S(2)}) copy-start(bf16[4,4,32,384]{3,2,1,0:T(8,128)(2,1)} %get-tuple-element.119) | copy-start | bytes 1179652
  280.7 3.8 %copy-start.44 = (bf16[4,4,32,384]{3,2,1,0:T(8,128)(2,1)S(1)}, bf16[4,4,32,384]{3,2,1,0:T(8,128)(2,1)}, u32[]{:S(2)}) copy-start(bf16[4,4,32,384]{3,2,1,0:T(8,128)(2,1)} %get-tuple-element.120) | copy-start | bytes 1179652
  280.7 3.8 %copy-start.61 = (bf16[384,1,192]{0,2,1:T(8,128)(2,1)S(1)}, bf16[384,1,192]{0,2,1:T(8,128)(2,1)}, u32[]{:S(2)}) copy-start(bf16[384,1,192]{0,2,1:T(8,128)(2,1)} %copy.130) | copy-start | bytes 442372
  280.8 4.2 %copy-start.59 = (bf16[384,1,192]{0,2,1:T(8,128)(2,1)S(1)}, bf16[384,1,192]{0,2,1:T(8,128)(2,1)}, u32[]{:S(2)}) copy-start(bf16[384,1,192]{0,2,1:T(8,128)(2,1)} %copy.131) | copy-start | bytes 442372
  282.1 3.2 copy-start.42
  282.1 3.2 copy-start.57
  286.3 1.1 copy-start.66
  287.7 1.1 copy-start.62
  288.8 1.1 copy-start.56
  289.2 1.1 copy-start.54
  290.2 1.1 copy-start.49
  295.5 9.6 %copy-start.94 = (f32[96]{0:T(128)S(1)}, f32[96]{0:T(128)}, u32[]{:S(2)}) copy-start(f32[96]{0:T(128)} %param.19) | copy-start | bytes 1156
  298.3 9.8 %collective-permute-start.4 = (bf16[4,1,64,192]{3,2,1,0:T(8,128)(2,1)}, bf16[4,1,64,192]{3,2,1,0:T(8,128)(2,1)S(1)}, u32[]{:S(2)}, u32[]{:S(2)}) collective-permute-start(bf16[4,1,64,192]{3,2,1,0:T(8,128)(2,1)} %get-tuple-element.125), channel_id=1, source_target_pairs={{0,1},{1,2},{2,3},{3,4},{4,5},{5,6},{6,7},{8,9},{9,10},{10,11},{11... | collective-permute-start | bytes 294920 | tf_op jit(solution)/shard_map/ppermute | solution.py:19
  301.9 6.5 %collective-permute-start.5 = (bf16[4,1,64,192]{3,2,1,0:T(8,128)(2,1)}, bf16[4,1,64,192]{3,2,1,0:T(8,128)(2,1)S(1)}, u32[]{:S(2)}, u32[]{:S(2)}) collective-permute-start(bf16[4,1,64,192]{3,2,1,0:T(8,128)(2,1)} %get-tuple-element.126), channel_id=1, source_target_pairs={{1,0},{2,1},{3,2},{4,3},{5,4},{6,5},{7,6},{9,8},{10,9},{11,10},{12... | collective-permute-start | bytes 294920 | tf_op jit(solution)/shard_map/ppermute | solution.py:21
  321.9 1.2 copy-start.16
  321.9 1.2 copy-start.74
  322.4 1.3 copy-start.15
  322.4 1.3 copy-start.73
  323.2 1.3 copy-start.14
  323.7 1.3 copy-start.13
  324.5 1.3 copy-start.12
  325.0 1.3 copy-start.11
  325.8 1.3 copy-start.10
  326.3 1.4 copy-start.9
  327.3 1.4 copy-start.8
  328.3 1.4 copy-start.7
  329.2 1.4 copy-start.6
  330.2 1.4 copy-start.5
  331.2 1.4 copy-start.4
  332.2 1.4 copy-start.3
  333.1 1.4 copy-start.2
  339.1 1.2 copy-start.17
  339.1 1.2 copy-start.77
  339.6 1.2 copy-start.76
  343.3 2.0 copy-start.1
  (55 other events, 57.8 us)
Sparse Core Ops, SparseCore 0:
  10.3 95.0 all-gather.1
where the time goes:
time: 359 us; the launch traced here: 352 us
  local copies, waits for them, and re-layouts  208 us (58%)
  starting transfers between devices  46.8 us (13%)
  blocking collectives  37.3 us (10%)
  matrix products  27.2 us (8%)
  between operations  18.1 us (5%)
  other arithmetic  9.07 us (3%)
  waiting for transfers between devices  5.1 us (1%)
    gather x256, local copies, waits for them, and re-layouts  94.3 us
    unnamed x219, local copies, waits for them, and re-layouts  51.6 us
    all_gather x1, blocking collectives, per_device(): lax.all_gather(w_out, 'grp', axis=0, tiled=True)  37.3 us
    slice x4, local copies, waits for them, and re-layouts, causal_conv(): weight[:, tap_index, :]  29.1 us
    dot_general x81, matrix products, causal_conv(): jnp.dot(window, weight[:, tap_index, :], preferred_element_type=jnp.float32)  27.2 us
    ppermute x3, starting transfers between devices, extended_2(): lax.ppermute(tail, axis, [(i, (i + 1) % count) for i in range(ends)])  23.3 us
    all_to_all x1, starting transfers between devices, per_device(): lax.all_to_all(outgoing, 'grp', split_axis=0, concat_axis=0, tiled=True)  17.2 us
    slice x6, local copies, waits for them, and re-layouts, causal_conv(): padded[time_tap:time_tap + count_t, row_tap:row_tap + count_r, col_tap:co...  15.8 us
  transfers between devices with their start and end apart: 8, of which 2 were waited for; matrix products, arithmetic and copies ran while one was open for 35% of the time, Pallas kernels for 0%

commit v1 on v0

v1 whole, which is shorter than its diff:
```python
import jax
import jax.numpy as jnp
from jax import lax
from jax.experimental import pallas as pl
from jax.experimental.pallas import tpu as pltpu
from jax.sharding import PartitionSpec as P

RL = 2
WL = 16
FMAX = 4
C1 = 384
C2 = 192
C3 = 96
C1P = 512
NB = 1792
EPS = 1e-06
F32 = jnp.float32
BF16 = jnp.bfloat16


def silu_norm(h, gain, width):
    mean_sq = jnp.sum(h * h, axis=-1, keepdims=True) * (1.0 / width)
    v = h * lax.rsqrt(mean_sq + EPS) * gain
    return v / (1.0 + jnp.exp(-v))


def iota(shape, dim):
    return lax.broadcasted_iota(jnp.int32, shape, dim)


def decode_kernel(
    info, xt_ref, win_ref, wmid_ref, wout_ref, gin_ref, gmid_ref, gout_ref, o_ref,
    cols, act1, z1, act2, z2, flat,
):
    row = info[0]
    count = info[1]

    xt = xt_ref[...].astype(F32)
    lane = iota(xt.shape, 1) % WL
    shifted = (
        jnp.where(lane == WL - 1, 0.0, xt),
        xt,
        jnp.where(lane == 0, 0.0, xt),
    )
    width = xt.shape[1]
    for a in range(3):
        for b in range(3):
            for e in range(3):
                start = 320 + (a - 2) * 96 + (b - 1) * 16 + (e - 1)
                piece = pltpu.roll(shifted[e], width - start, 1)[:, :384]
                k = 9 * a + 3 * b + e
                cols[16 * k : 16 * k + 16, :] = piece.astype(BF16)
    h = lax.dot_general(
        cols[...], win_ref[...], (((0,), (0,)), ((), ())), preferred_element_type=F32
    )
    act = silu_norm(h, gin_ref[...], C1).astype(BF16)
    src = iota((C1, C1P), 0)
    dst = iota((C1, C1P), 1)
    place = ((dst // 8 * 6 + dst % 8 == src) & (dst % 8 < 6)).astype(F32).astype(BF16)
    spread = jnp.dot(act, place, preferred_element_type=F32)
    act1[0:128, :] = jnp.zeros((128, C1P), BF16)
    rid = 2 * row - 1 + iota((64, 1), 0) // WL
    keep = (rid >= 0) & (rid < 16)
    for t in range(FMAX):
        part = spread[t * 96 + 16 : t * 96 + 80, :]
        act1[128 + 64 * t : 192 + 64 * t, :] = jnp.where(keep, part, 0.0).astype(BF16)

    for a in range(3):
        part = jnp.dot(
            act1[64 * a : 64 * a + 256, :],
            wmid_ref[:, NB * a : NB * a + NB],
            preferred_element_type=F32,
        )
        if a == 0:
            z1[...] = part
        else:
            z1[...] += part

    act2[0:384, :] = jnp.zeros((384, C2), BF16)
    xpos = iota((64, 1), 0) % WL
    gmid = gmid_ref[...]
    for t in range(FMAX):
        combos = []
        for b in range(3):
            z = []
            for e in range(3):
                k = 3 * b + e
                if k % 2 == 0:
                    z.append(z1[64 * t : 64 * t + 64, 192 * k : 192 * k + 192])
                else:
                    win = z1[64 * t : 64 * t + 64, 192 * k - 64 : 192 * k + 192]
                    z.append(pltpu.roll(win, 192, 1)[:, :192])
            left = jnp.where(xpos == 0, 0.0, pltpu.roll(z[0], 1, 0))
            right = jnp.where(xpos == WL - 1, 0.0, pltpu.roll(z[2], 63, 0))
            combos.append((left + z[1] + z[2], z[0] + z[1] + right))
        for m in range(6):
            y, p = (m + 1) // 2, (m + 1) % 2
            rows = (y, y, y + 1) if p else (y - 1, y, y)
            rid2 = 4 * row - 1 + m
            ok = (rid2 >= 0) & (rid2 < 32)
            for q in range(2):
                h = sum(combos[b][q][16 * rows[b] : 16 * rows[b] + 16, :] for b in range(3))
                v = jnp.where(ok, silu_norm(h, gmid, C2), 0.0)
                at = ((t + 2) * 12 + m * 2 + q) * 16
                act2[at : at + 16, :] = v.astype(BF16)

    for a in range(3):
        part = jnp.dot(
            act2[192 * a : 192 * a + 768, :], wout_ref[a], preferred_element_type=F32
        )
        if a == 0:
            z2[...] = part
        else:
            z2[...] += part

    xpos = iota((96, 1), 0) % WL
    gout = gout_ref[...]
    lanes = iota((64, 128), 1)
    for t in range(FMAX):
        combos = []
        for b in range(3):
            z = []
            for e in range(3):
                k = 3 * b + e
                block = z2[192 * t : 192 * t + 192, 128 * k : 128 * k + 128].reshape(6, 2, 16, 128)
                z.append((block[:, 0].reshape(96, 128), block[:, 1].reshape(96, 128)))
            left = (jnp.where(xpos == 0, 0.0, pltpu.roll(z[0][1], 1, 0)), z[0][0])
            right = (z[2][1], jnp.where(xpos == WL - 1, 0.0, pltpu.roll(z[2][0], 95, 0)))
            combos.append(
                [
                    (left[q] + z[1][q] + z[2][q], z[0][q] + z[1][q] + right[q])
                    for q in range(2)
                ]
            )
        for p in range(2):
            phases = []
            for q in range(2):
                for q2 in range(2):
                    c = [combos[b][q][q2] for b in range(3)]
                    if p:
                        h = c[0][16:80] + c[1][16:80] + c[2][32:96]
                    else:
                        h = c[0][0:64] + c[1][16:80] + c[2][16:80]
                    phases.append(jnp.where(t < count, silu_norm(h, gout, C3), 0.0))
            r1 = pltpu.roll(phases[1], 96, 1)
            r2 = pltpu.roll(phases[2], 64, 1)
            r3 = pltpu.roll(phases[3], 32, 1)
            tiles = (
                jnp.where(lanes < 96, phases[0], r1),
                jnp.where(lanes < 64, r1, r2),
                jnp.where(lanes < 32, r2, r3),
            )
            for m in range(4):
                at = (t * 8 + 2 * m + p) * 16
                for j in range(3):
                    flat[j, at : at + 16, :] = tiles[j][16 * m : 16 * m + 16]
        for x in range(WL):
            for j in range(3):
                v = flat[j, pl.ds(t * 128 + x, 8, stride=16), :]
                at = x * 384 + j * 128
                o_ref[0, t, :, at : at + 128] = v.astype(BF16)


def decode(info, xt, win, wmid, wout, gin, gmid, gout):
    vm = pl.BlockSpec(memory_space=pltpu.VMEM)
    return pl.pallas_call(
        decode_kernel,
        name="decode",
        out_shape=jax.ShapeDtypeStruct((1, FMAX, 4 * RL, 4 * WL * C3), BF16),
        in_specs=[pl.BlockSpec(memory_space=pltpu.SMEM)] + [vm] * 7,
        out_specs=vm,
        scratch_shapes=[
            pltpu.VMEM((432, 384), BF16),
            pltpu.VMEM((384, C1P), BF16),
            pltpu.VMEM((256, NB), F32),
            pltpu.VMEM((1152, C2), BF16),
            pltpu.VMEM((768, 1152), F32),
            pltpu.VMEM((3, 512, 128), F32),
        ],
        compiler_params=pltpu.CompilerParams(vmem_limit_bytes=48 * 1024 * 1024),
    )(info, xt, win, wmid, wout, gin, gmid, gout)


def per_device(latents, frames, offsets, assign, w_in, w_mid, w_out, gain_in, gain_mid, gain_out):
    groups = lax.axis_size("grp")
    row_index = lax.axis_index("row")
    group_index = lax.axis_index("grp")
    channels = w_in.shape[0]
    cap_vals = latents.shape[1] // groups
    cap_tokens = cap_vals // channels
    span_len = cap_tokens // FMAX

    mid = w_mid.reshape(6, 3, 9 * C2)
    mid = jnp.pad(mid, ((0, 2), (0, 0), (0, NB - 9 * C2))).reshape(8, 3 * NB)
    full_mid = lax.all_gather(mid, "grp", axis=0, tiled=True)
    full_out = lax.all_gather(w_out, "grp", axis=0, tiled=True)
    wout = jnp.pad(full_out, ((0, 0), (0, 0), (0, 128 - C3)))
    wout = wout.reshape(C2, 3, 9 * 128).transpose(1, 0, 2)
    win = w_in.transpose(1, 0, 2).reshape(27 * channels, C1)

    table = latents.reshape(128, 128)
    start = offsets[assign]
    length = frames[assign] * (span_len * channels)
    first = start // 8
    want = first[:, None] + jnp.arange(3, dtype=jnp.int32)[None, :]
    pick = (want.reshape(-1)[:, None] == jnp.arange(128, dtype=jnp.int32)[None, :]).astype(BF16)
    rows = jnp.dot(pick, table, preferred_element_type=F32).astype(BF16).reshape(groups, 384)
    shift = (start % 8)[:, None]
    for bit in (4, 2, 1):
        moved = jnp.pad(rows[:, 16 * bit :], ((0, 0), (0, 16 * bit)))
        rows = jnp.where((shift & bit) != 0, moved, rows)
    keep = jnp.arange(cap_vals, dtype=jnp.int32)[None, :] < length[:, None]
    outgoing = jnp.where(keep, rows[:, :cap_vals], jnp.zeros((), BF16))
    incoming = lax.all_to_all(outgoing, "grp", split_axis=0, concat_axis=0, tiled=True)

    tokens = incoming.reshape(groups * cap_tokens, channels)
    request = assign[group_index]
    count = frames[request]
    fill_len = count * span_len
    frame_ids = jnp.arange(FMAX, dtype=jnp.int32)[:, None, None]
    row_ids = row_index * RL - 2 + jnp.arange(6, dtype=jnp.int32)[None, :, None]
    col_ids = jnp.arange(WL, dtype=jnp.int32)[None, None, :]
    position = (frame_ids * 16 + row_ids) * WL + col_ids
    valid = (row_ids >= 0) & (row_ids < 16) & (frame_ids < count) & (col_ids >= 0)
    position = jnp.where(valid, position, 0)
    shard = jnp.minimum(position // fill_len, groups - 1)
    within = position % fill_len
    picked = tokens[(shard * cap_tokens + within).reshape(-1)]
    picked = jnp.where(valid.reshape(-1, 1), picked, jnp.zeros((), BF16))
    xt = jnp.pad(picked.T, ((0, 0), (320, 64)))
    info = jnp.stack([row_index.astype(jnp.int32), count])
    gout = jnp.pad(gain_out, (0, 128 - C3)).reshape(1, 128)
    return decode(
        info, xt, win, full_mid, wout, gain_in.reshape(1, C1), gain_mid.reshape(1, C2), gout
    )


def solution(mesh):
    placed = (
        P("grp", None),
        P(),
        P(),
        P(),
        P(),
        P("grp", None, None),
        P("grp", None, None),
        P(),
        P(),
        P(),
    )
    return jax.shard_map(
        per_device,
        mesh=mesh,
        in_specs=placed,
        out_specs=P("grp", None, "row", None),
        check_vma=False,
    )
```

time: 359 us -> 122 us (0.34); the launches traced: 352 us -> 120 us
  local copies, waits for them, and re-layouts: 208 us -> 13.7 us
  starting transfers between devices: 46.8 us -> 17.2 us
  matrix products: 27.2 us -> 0.21 us
  waiting for transfers between devices: 5.1 us -> 16.5 us
  Pallas kernels: 0 us -> 9.07 us
  blocking collectives: 37.3 us -> 43.3 us
  other arithmetic: 9.07 us -> 4.22 us
    gather x259 -> x4, local copies, waits for them, and re-layouts: 97.2 us -> 3.73 us  [the longest x2 1.52 us: per_device(): picked = tokens[(shard * cap_tokens + within).reshape(-1)]]
    unnamed x219 -> x19, local copies, waits for them, and re-layouts: 51.6 us -> 2.87 us
    slice x13 -> x3, local copies, waits for them, and re-layouts: 45.6 us -> 0.25 us  [per_device(): moved = jnp.pad(rows[:, 16 * bit:], ((0, 0), (0, 16 * bit)))]
    ppermute x6 -> x0, starting transfers between devices: 29.5 us -> none  [the longest x3 23.3 us: extended_2(): lax.ppermute(tail, axis, [(i, (i + 1) % count) for i in range(ends)])]
    dot_general x81 -> x1, matrix products: 27.2 us -> 0.21 us  [per_device(): jnp.dot(pick, table, preferred_element_type=F32).astype(BF16)]
    all_gather x1, waiting for transfers between devices: 0.02 us -> 16.5 us  [per_device(): full_mid = lax.all_gather(mid, 'grp', axis=0, tiled=True)]
    pallas_call x0 -> x1, Pallas kernels: none -> 9.07 us  [decode(): pl.pallas_call(decode_kernel, name='decode', out_shape=jax.ShapeDtypeStru...]
    all_gather x1, blocking collectives: 37.3 us -> 43.3 us  [per_device(): full_out = lax.all_gather(w_out, 'grp', axis=0, tiled=True)]
  transfers between devices with their start and end apart: 8 -> 2, of which waited for: 2 -> 1; matrix products, arithmetic and copies ran while one was open for 35% -> 14% of each run, Pallas kernels for 0% -> 0%
where the time goes in v1:
time: 122 us; the launch traced here: 120 us
  blocking collectives  43.3 us (35%)
  starting transfers between devices  17.2 us (14%)
  waiting for transfers between devices  16.5 us (14%)
  between operations  16 us (13%)
  local copies, waits for them, and re-layouts  13.7 us (11%)
  Pallas kernels  9.07 us (7%)
  other arithmetic  4.22 us (3%)
    all_gather x1, blocking collectives, per_device(): full_out = lax.all_gather(w_out, 'grp', axis=0, tiled=True)  43.3 us
    all_to_all x1, starting transfers between devices, per_device(): lax.all_to_all(outgoing, 'grp', split_axis=0, concat_axis=0, tiled=True)  17.1 us
    all_gather x1, waiting for transfers between devices, per_device(): full_mid = lax.all_gather(mid, 'grp', axis=0, tiled=True)  16.5 us
    pallas_call x1, Pallas kernels, decode(): pl.pallas_call(decode_kernel, name='decode', out_shape=jax.ShapeDtypeStru...  9.07 us
    unnamed x19, local copies, waits for them, and re-layouts  2.87 us
  transfers between devices with their start and end apart: 2, of which 1 were waited for; matrix products, arithmetic and copies ran while one was open for 14% of the time, Pallas kernels for 0%

profile of v1, /device:TPU:1, one launch (start us, length us, event | category | flops | bytes accessed | tf_op | source)
XLA Modules:
  0.0 120.3 jit_solution(14814448195893503600)
XLA Ops:
  6.5 0.0 all-gather.2.cloned.1.call-start
  6.6 1.1 reshape.303
  7.7 0.7 pad.32
  8.3 0.0 all-gather.2.cloned.1.call-update
  8.3 0.7 compare_select_fusion.1
  9.0 1.4 %gather_fusion.1 = s32[64]{0:T(128)S(1)} fusion(s32[64]{0:T(128)} %param.12, s32[1024]{0:T(1024)S(1)} %pad_clamp_fusion.1), kind=kCustom, calls=%fused_computation.1 | custom fusion | bytes 768 | tf_op jit(solution)/shard_map/gather | solution.py:202
  10.5 0.1 iota_add_fusion
  10.5 0.1 add.176
  10.7 0.2 reduce
  10.9 0.2 convolution_convert_fusion
  11.1 0.1 slice.22
  11.2 0.1 pad_select_fusion.1
  11.3 0.1 slice.23
  11.4 0.1 pad_select_fusion
  11.5 0.1 slice.24
  11.6 0.8 gather_fusion
  12.4 0.1 fusion.2
  12.5 0.5 broadcast.434
  13.0 0.6 reduce.4
  13.6 0.6 reshape.339
  14.2 17.1 %all-to-all-start = ((bf16[64,2,128]{2,1,0:T(2,128)(2,1)}), bf16[64,2,128]{2,1,0:T(2,128)(2,1)S(1)}, u32[]{:S(2)}, u32[]{:S(2)}) async-start(bf16[64,2,128]{2,1,0:T(2,128)(2,1)} %reshape.339), calls=%async_computation | async-start | bytes 65536 | tf_op jit(solution)/shard_map/all_to_all | solution.py:214
  31.3 0.6 dynamic_slice.6
  33.6 0.6 dynamic_slice.7
  34.9 0.6 iota_compare_fusion.3
  35.5 0.1 broadcast_and_fusion
  35.6 0.1 add_multiply_fusion
  35.7 0.4 fusion.5
  36.1 0.1 div.34
  36.2 0.1 rem.77
  36.3 0.3 fusion.6
  36.6 0.1 reshape.309
  36.7 0.1 and.138
  36.7 0.1 and.139
  36.8 43.3 %all_gather.7 = bf16[192,27,96]{2,1,0:T(8,128)(2,1)S(1)} all-gather(bf16[3,27,96]{2,1,0:T(8,128)(2,1)S(1)} %copy-done.4), channel_id=1, replica_groups=mesh['grp'=64,'row'=8] {'grp'}, dimensions={0}, use_global_device_ids=true | all-gather | bytes 1010880 | tf_op jit(solution)/shard_map/all_gather | solution.py:196
  80.2 2.2 %copy.26 = bf16[192,27,96]{0,2,1:T(8,128)(2,1)} copy(bf16[192,27,96]{2,1,0:T(8,128)(2,1)S(1)} %all_gather.7) | data formatting | bytes 1990656
  82.4 1.6 %pad.33.clone = bf16[192,27,128]{0,2,1:T(8,128)(2,1)S(1)} pad(bf16[192,27,96]{0,2,1:T(8,128)(2,1)} %copy.26, bf16[]{:T(256)} %constant.77.clone.1), padding=0_0x0_0x0_32 | pad | bytes 2322434 | tf_op jit(solution)/shard_map/jit(_pad)/pad | solution.py:197
  84.0 0.0 copy-start.5
  84.0 0.0 copy-start.7
  84.0 0.0 copy-start.1
  84.0 0.9 copy.25
  85.0 0.7 pad_add_fusion.info
  85.8 0.2 reduce.1
  86.0 0.2 reshape.301
  86.2 1.4 %gather_fusion.2 = bf16[384,16]{1,0:T(8,128)(2,1)S(1)} fusion(bf16[1024,16]{1,0:T(8,128)(2,1)S(1)} %reshape.301, s32[1024]{0:T(1024)S(1)} %pad_clamp_fusion), kind=kCustom, calls=%fused_computation.2 | custom fusion | bytes 26112 | tf_op jit(solution)/shard_map/gather | solution.py:228
  87.7 0.1 copy.22
  87.8 0.1 pad.31.xt_ref
  87.8 16.5 %all-gather.2.cloned.1.call-done.wmid_ref = bf16[512,5376]{1,0:T(8,128)(2,1)} async-done(((bf16[8,5376]{1,0:T(8,128)(2,1)}), bf16[512,5376]{1,0:T(8,128)(2,1)}) %all-gather.2.cloned.1.call-update) | async-done | bytes 5505040 | tf_op jit(solution)/shard_map/all_gather | solution.py:195
  104.4 9.1 %decode.1 = bf16[1,4,8,6144]{3,2,1,0:T(8,128)(2,1)} custom-call(s32[2]{0:T(128)S(1)} %pad_add_fusion.info, bf16[16,768]{1,0:T(8,128)(2,1)S(1)} %pad.31.xt_ref, bf16[432,384]{1,0:T(8,128)(2,1)S(1)} %bitcast.20, bf16[512,5376]{1,0:T(8,128)(2,1)} %all-gather.2.cloned.1.call-done.wmid_ref, bf16[3,192,1152]{2,1,0:T(8,128)(2,1)S(1)} %bitcast.19, ...), custom_call_target="tpu_custom_call" | custom-call | tf_op jit(solution)/shard_map/decode/pallas_call | solution.py:166
  (30 shorter events, 0.2 us)
Async XLA Ops:
  6.5 4.1 %copy-start = (bf16[1,16384]{1,0:T(2,128)(2,1)S(1)}, bf16[1,16384]{1,0:T(2,128)(2,1)}, u32[]{:S(2)}) copy-start(bf16[1,16384]{1,0:T(2,128)(2,1)} %param.10) | copy-start | bytes 98308
  6.5 24.8 %copy-start.6 = (s32[64]{0:T(128)S(1)}, s32[64]{0:T(128)}, u32[]{:S(2)}) copy-start(s32[64]{0:T(128)} %param.13) | copy-start | bytes 772
  6.5 5.1 %copy-start.3 = (s32[64]{0:T(128)S(1)}, s32[64]{0:T(128)}, u32[]{:S(2)}) copy-start(s32[64]{0:T(128)} %param.11) | copy-start | bytes 772
  6.5 30.3 %copy-start.4 = (bf16[3,27,96]{2,1,0:T(8,128)(2,1)S(1)}, bf16[3,27,96]{2,1,0:T(8,128)(2,1)}, u32[]{:S(2)}) copy-start(bf16[3,27,96]{2,1,0:T(8,128)(2,1)} %param.16) | copy-start | bytes 46660
  6.5 97.8 %all-gather.2.cloned.1.call-start = ((), (), s32[]{:S(2)}) async-start(), calls=%async_computation.1 | async-start | bytes 5591040 | tf_op jit(solution)/shard_map/all_gather | solution.py:195
  14.2 71.6 %all-to-all-start = ((bf16[64,2,128]{2,1,0:T(2,128)(2,1)}), bf16[64,2,128]{2,1,0:T(2,128)(2,1)S(1)}, u32[]{:S(2)}, u32[]{:S(2)}) async-start(bf16[64,2,128]{2,1,0:T(2,128)(2,1)} %reshape.339), calls=%async_computation | async-start | bytes 65536 | tf_op jit(solution)/shard_map/all_to_all | solution.py:214
  84.0 1.0 copy-start.5
  84.0 1.7 %copy-start.7 = (f32[96]{0:T(128)S(1)}, f32[96]{0:T(128)}, u32[]{:S(2)}) copy-start(f32[96]{0:T(128)} %param.19) | copy-start | bytes 1156
  84.0 20.4 %copy-start.1 = (bf16[16,27,384]{2,0,1:T(8,128)(2,1)S(1)}, bf16[16,27,384]{2,0,1:T(8,128)(2,1)}, u32[]{:S(2)}) copy-start(bf16[16,27,384]{2,0,1:T(8,128)(2,1)} %param.14) | copy-start | bytes 995332
  84.0 20.3 %copy-start.2 = (f32[192]{0:T(256)S(1)}, f32[192]{0:T(256)}, u32[]{:S(2)}) copy-start(f32[192]{0:T(256)} %param.18) | copy-start | bytes 2308
Sparse Core Ops, SparseCore 0:
  10.4 93.9 all-gather.1

commit v2 on v1

--- a/solution.py
+++ b/solution.py
@@ -13,9 +13,18 @@
 C3 = 96
 C1P = 512
 NB = 1792
+MIDH = 3 * NB // 2
+HALF = MIDH + 9 * 128
+MID_PARTS = (
+    (0, 0, 0, 0, NB),
+    (1, 0, NB, 0, NB // 2),
+    (1, 1, 0, NB // 2, NB // 2),
+    (2, 1, NB // 2, 0, NB),
+)
 EPS = 1e-06
 F32 = jnp.float32
 BF16 = jnp.bfloat16
+MESH = pl.DeviceIdType.MESH
 
 
 def silu_norm(h, gain, width):
@@ -29,8 +38,8 @@
 
 
 def decode_kernel(
-    info, xt_ref, win_ref, wmid_ref, wout_ref, gin_ref, gmid_ref, gout_ref, o_ref,
-    cols, act1, z1, act2, z2, flat,
+    info, xt_ref, win_ref, w_ref, gin_ref, gmid_ref, gout_ref, o_ref,
+    cols, act1, z1, act2, lhs, z2, flat,
 ):
     row = info[0]
     count = info[1]
@@ -65,16 +74,16 @@
         part = spread[t * 96 + 16 : t * 96 + 80, :]
         act1[128 + 64 * t : 192 + 64 * t, :] = jnp.where(keep, part, 0.0).astype(BF16)
 
-    for a in range(3):
+    for a, half, start, at, size in MID_PARTS:
         part = jnp.dot(
             act1[64 * a : 64 * a + 256, :],
-            wmid_ref[:, NB * a : NB * a + NB],
+            w_ref[half, :, start : start + size],
             preferred_element_type=F32,
         )
         if a == 0:
-            z1[...] = part
+            z1[:, at : at + size] = part
         else:
-            z1[...] += part
+            z1[:, at : at + size] += part
 
     act2[0:384, :] = jnp.zeros((384, C2), BF16)
     xpos = iota((64, 1), 0) % WL
@@ -104,14 +113,17 @@
                 at = ((t + 2) * 12 + m * 2 + q) * 16
                 act2[at : at + 16, :] = v.astype(BF16)
 
-    for a in range(3):
-        part = jnp.dot(
-            act2[192 * a : 192 * a + 768, :], wout_ref[a], preferred_element_type=F32
-        )
-        if a == 0:
-            z2[...] = part
-        else:
-            z2[...] += part
+    src = iota((C2, 512), 0)
+    dst = iota((C2, 512), 1)
+    low = ((dst // 8 * 3 + dst % 8 == src) & (dst % 8 < 3)).astype(F32).astype(BF16)
+    high = ((dst // 8 * 3 + dst % 8 - 4 == src) & (dst % 8 >= 4) & (dst % 8 < 7)).astype(F32)
+    high = high.astype(BF16)
+    both = jnp.dot(act2[0:768, :], low, preferred_element_type=F32)
+    both += jnp.dot(act2[192:960, :], high, preferred_element_type=F32)
+    lhs[0] = both.astype(BF16)
+    lhs[1] = jnp.dot(act2[384:1152, :], low, preferred_element_type=F32).astype(BF16)
+    z2[...] = jnp.dot(lhs[0], w_ref[0, :, MIDH:HALF], preferred_element_type=F32)
+    z2[...] += jnp.dot(lhs[1], w_ref[1, :, MIDH:HALF], preferred_element_type=F32)
 
     xpos = iota((96, 1), 0) % WL
     gout = gout_ref[...]
@@ -161,24 +173,140 @@
                 o_ref[0, t, :, at : at + 128] = v.astype(BF16)
 
 
-def decode(info, xt, win, wmid, wout, gin, gmid, gout):
+def decode(info, xt, win, weights, gin, gmid, gout):
     vm = pl.BlockSpec(memory_space=pltpu.VMEM)
     return pl.pallas_call(
         decode_kernel,
         name="decode",
         out_shape=jax.ShapeDtypeStruct((1, FMAX, 4 * RL, 4 * WL * C3), BF16),
-        in_specs=[pl.BlockSpec(memory_space=pltpu.SMEM)] + [vm] * 7,
+        in_specs=[pl.BlockSpec(memory_space=pltpu.SMEM)] + [vm] * 6,
         out_specs=vm,
         scratch_shapes=[
             pltpu.VMEM((432, 384), BF16),
             pltpu.VMEM((384, C1P), BF16),
             pltpu.VMEM((256, NB), F32),
             pltpu.VMEM((1152, C2), BF16),
+            pltpu.VMEM((2, 768, 512), BF16),
             pltpu.VMEM((768, 1152), F32),
             pltpu.VMEM((3, 512, 128), F32),
         ],
-        compiler_params=pltpu.CompilerParams(vmem_limit_bytes=48 * 1024 * 1024),
-    )(info, xt, win, wmid, wout, gin, gmid, gout)
+        compiler_params=pltpu.CompilerParams(vmem_limit_bytes=56 * 1024 * 1024),
+    )(info, xt, win, weights, gin, gmid, gout)
+
+
+def gather_kernel(x_ref, g_ref, own_sem, send_sem, recv_sem):
+    grp = lax.axis_index("grp")
+    row = lax.axis_index("row")
+    core = row % 2
+    step1 = 1 + 7 * core
+    step2 = 8 - 7 * core
+    i1 = (grp // step1) % 8
+    i2 = (grp // step2) % 8
+
+    def slot(a, b):
+        return (a % 8) * step1 + (b % 8) * step2
+
+    right1, left1 = (slot(i1 + 1, i2), row), (slot(i1 + 7, i2), row)
+    right2, left2 = (slot(i1, i2 + 1), row), (slot(i1, i2 + 7), row)
+    partner = (grp, row + 1 - 2 * core)
+
+    barrier = pltpu.get_barrier_semaphore()
+    for peer in (right1, left1, right2, left2, partner):
+        pl.semaphore_signal(barrier, inc=1, device_id=peer, device_id_type=MESH)
+    pl.semaphore_wait(barrier, 5)
+
+    started = []
+
+    def send(way, peer, a, b, own=False):
+        at = slot(a, b)
+        copy = pltpu.make_async_remote_copy(
+            src_ref=x_ref.at[core] if own else g_ref.at[core, at],
+            dst_ref=g_ref.at[core, at],
+            send_sem=send_sem.at[way, at],
+            recv_sem=recv_sem.at[core, at],
+            device_id=peer,
+            device_id_type=MESH,
+        )
+        copy.start()
+        started.append(copy)
+
+    def arrived(half, at):
+        pltpu.make_async_remote_copy(
+            src_ref=g_ref.at[half, at],
+            dst_ref=g_ref.at[half, at],
+            send_sem=send_sem.at[0, at],
+            recv_sem=recv_sem.at[half, at],
+            device_id=partner,
+            device_id_type=MESH,
+        ).wait_recv()
+
+    send(0, right1, i1, i2, True)
+    send(1, left1, i1, i2, True)
+    send(2, right2, i1, i2, True)
+    send(3, left2, i1, i2, True)
+    local = [
+        pltpu.make_async_copy(x_ref.at[h], g_ref.at[h, grp], own_sem.at[h]) for h in range(2)
+    ]
+    for copy in local:
+        copy.start()
+
+    line = [0, -1, 1, -2, 2, -3, 3, -4]
+    for off in line[1:]:
+        arrived(core, slot(i1 + off + 8, i2))
+        if -4 < off < 0:
+            send(0, right1, i1 + off + 8, i2)
+        if 0 < off < 3:
+            send(1, left1, i1 + off + 8, i2)
+        send(2, right2, i1 + off + 8, i2)
+        send(3, left2, i1 + off + 8, i2)
+        send(4, partner, i1 + off + 8, i2)
+
+    for dist in range(1, 5):
+        for n, off in enumerate(line):
+            a = i1 + off + 8
+            for sign in (-1, 1):
+                if dist == 4 and (n % 2 == 0) != (sign < 0):
+                    continue
+                b = i2 + sign * dist + 8
+                arrived(core, slot(a, b))
+                if dist < 3 or (dist == 3 and (n % 2 == 0) == (sign < 0)):
+                    send(2 if sign < 0 else 3, right2 if sign < 0 else left2, a, b)
+                send(4, partner, a, b)
+
+    for n in range(1, 64):
+        arrived(1 - core, (grp + n) % 64)
+    for copy in started:
+        copy.wait_send()
+    for copy in local:
+        copy.wait()
+
+
+def gather_weights(x):
+    any_spec = pl.BlockSpec(memory_space=pl.ANY)
+    return pl.pallas_call(
+        gather_kernel,
+        name="gather",
+        out_shape=jax.ShapeDtypeStruct((2, 64, 8, HALF), BF16),
+        in_specs=[any_spec],
+        out_specs=any_spec,
+        scratch_shapes=[
+            pltpu.SemaphoreType.DMA((2,)),
+            pltpu.SemaphoreType.DMA((5, 64)),
+            pltpu.SemaphoreType.DMA((2, 64)),
+        ],
+        compiler_params=pltpu.CompilerParams(collective_id=0, has_side_effects=True),
+    )(x)
+
+
+def pack_weights(w_mid, w_out):
+    mid = w_mid.reshape(6, 3, 9 * C2)
+    mid = jnp.pad(mid, ((0, 2), (0, 0), (0, NB - 9 * C2))).reshape(8, 3 * NB)
+    out = jnp.pad(w_out, ((0, 0), (0, 0), (0, 128 - C3))).reshape(3, 3, 9 * 128)
+    out = jnp.pad(out.transpose(1, 0, 2), ((0, 1), (0, 1), (0, 0))).reshape(2, 8, 9 * 128)
+    halves = [
+        jnp.concatenate([mid[:, h * MIDH : (h + 1) * MIDH], out[h]], axis=1) for h in range(2)
+    ]
+    return jnp.stack(halves)
 
 
 def per_device(latents, frames, offsets, assign, w_in, w_mid, w_out, gain_in, gain_mid, gain_out):
@@ -190,12 +318,7 @@
     cap_tokens = cap_vals // channels
     span_len = cap_tokens // FMAX
 
-    mid = w_mid.reshape(6, 3, 9 * C2)
-    mid = jnp.pad(mid, ((0, 2), (0, 0), (0, NB - 9 * C2))).reshape(8, 3 * NB)
-    full_mid = lax.all_gather(mid, "grp", axis=0, tiled=True)
-    full_out = lax.all_gather(w_out, "grp", axis=0, tiled=True)
-    wout = jnp.pad(full_out, ((0, 0), (0, 0), (0, 128 - C3)))
-    wout = wout.reshape(C2, 3, 9 * 128).transpose(1, 0, 2)
+    weights = gather_weights(pack_weights(w_mid, w_out)).reshape(2, 8 * groups, HALF)
     win = w_in.transpose(1, 0, 2).reshape(27 * channels, C1)
 
     table = latents.reshape(128, 128)
@@ -231,7 +354,7 @@
     info = jnp.stack([row_index.astype(jnp.int32), count])
     gout = jnp.pad(gain_out, (0, 128 - C3)).reshape(1, 128)
     return decode(
-        info, xt, win, full_mid, wout, gain_in.reshape(1, C1), gain_mid.reshape(1, C2), gout
+        info, xt, win, weights, gain_in.reshape(1, C1), gain_mid.reshape(1, C2), gout
     )
 
 

time: 122 us -> 96.7 us (0.79); the launches traced: 120 us -> 96.3 us
  Pallas kernels: 9.07 us -> 57 us
  blocking collectives: 43.3 us -> 0 us
  waiting for transfers between devices: 16.5 us -> 0.01 us
  between operations: 16 us -> 2.86 us
  other arithmetic: 4.22 us -> 5.62 us
    pallas_call x0 -> x1, Pallas kernels: none -> 45.9 us  [gather_weights(): pl.pallas_call(gather_kernel, name='gather', out_shape=jax.ShapeDtypeStru...]
    all_gather x1 -> x0, blocking collectives: 43.3 us -> none  [per_device(): full_out = lax.all_gather(w_out, 'grp', axis=0, tiled=True)]
    all_gather x1 -> x0, waiting for transfers between devices: 16.5 us -> none  [per_device(): full_mid = lax.all_gather(mid, 'grp', axis=0, tiled=True)]
    unnamed x19 -> x6, local copies, waits for them, and re-layouts: 2.87 us -> 0.64 us
    pallas_call x1, Pallas kernels: 9.07 us -> 11.1 us  [decode(): pl.pallas_call(decode_kernel, name='decode', out_shape=jax.ShapeDtypeStru...]
    pad x2, local copies, waits for them, and re-layouts: 2.27 us -> 0.78 us  [the longest x1 0.76 us: pack_weights(): out = jnp.pad(w_out, ((0, 0), (0, 0), (0, 128 - C3))).reshape(3, 3, 9 * 128)]
    reshape x1, local copies, waits for them, and re-layouts: 0.01 us -> 1.26 us  [per_device(): gain_in.reshape(1, C1)]
  transfers between devices with their start and end apart: 2 -> 1, of which waited for: 1 -> 0; matrix products, arithmetic and copies ran while one was open for 14% -> 11% of each run, Pallas kernels for 0% -> 48%
where the time goes in v2:
time: 96.7 us; the launch traced here: 96.3 us
  Pallas kernels  57 us (59%)
  starting transfers between devices  17.1 us (18%)
  local copies, waits for them, and re-layouts  13.5 us (14%)
  other arithmetic  5.62 us (6%)
  between operations  2.86 us (3%)
    pallas_call x1, Pallas kernels, gather_weights(): pl.pallas_call(gather_kernel, name='gather', out_shape=jax.ShapeDtypeStru...  45.9 us
    all_to_all x1, starting transfers between devices, per_device(): lax.all_to_all(outgoing, 'grp', split_axis=0, concat_axis=0, tiled=True)  17.1 us
    pallas_call x1, Pallas kernels, decode(): pl.pallas_call(decode_kernel, name='decode', out_shape=jax.ShapeDtypeStru...  11.1 us
  transfers between devices with their start and end apart: 1, of which 0 were waited for; matrix products, arithmetic and copies ran while one was open for 11% of the time, Pallas kernels for 48%

profile of v2, /device:TPU:1, one launch (start us, length us, event | category | flops | bytes accessed | tf_op | source)
XLA Modules:
  0.0 96.3 jit_solution(7069717508879894720)
XLA Ops:
  0.0 0.0 copy-start
  0.0 0.0 copy-start.1
  0.0 0.7 compare_select_fusion.1
  0.7 1.4 %gather_fusion.1 = s32[64]{0:T(128)S(1)} fusion(s32[64]{0:T(128)} %param.12, s32[1024]{0:T(1024)S(1)} %pad_clamp_fusion.1), kind=kCustom, calls=%fused_computation.1 | custom fusion | bytes 768 | tf_op jit(solution)/shard_map/gather | solution.py:325
  2.2 1.4 %gather_fusion = s32[64]{0:T(128)S(1)} fusion(s32[64]{0:T(128)} %param.11, s32[1024]{0:T(1024)S(1)} %pad_clamp_fusion.1), kind=kCustom, calls=%fused_computation | custom fusion | bytes 768 | tf_op jit(solution)/shard_map/gather | solution.py:326
  3.6 0.1 iota_add_fusion
  3.7 0.1 add.178
  3.8 0.0 copy-done
  3.8 0.2 reduce
  4.0 0.2 convolution_convert_fusion
  4.3 0.1 slice.40
  4.4 0.1 pad_select_fusion.1
  4.4 0.1 slice.41
  4.5 0.1 pad_select_fusion
  4.6 0.1 slice.42
  4.7 0.1 fusion.2
  4.8 0.5 broadcast.436
  5.3 0.7 reduce.4
  6.0 0.6 reshape.348
  6.6 17.1 %all-to-all-start = ((bf16[64,2,128]{2,1,0:T(2,128)(2,1)}), bf16[64,2,128]{2,1,0:T(2,128)(2,1)S(1)}, u32[]{:S(2)}, u32[]{:S(2)}) async-start(bf16[64,2,128]{2,1,0:T(2,128)(2,1)} %reshape.348), calls=%async_computation | async-start | bytes 65536 | tf_op jit(solution)/shard_map/all_to_all | solution.py:337
  23.7 1.2 %dynamic_slice.6 = s32[1]{0:T(128)} dynamic-slice(s32[64]{0:T(128)} %param.13, s32[]{:T(128)S(6)} %select_n.110), dynamic_slice_sizes={1} | dynamic-slice | bytes 12 | tf_op jit(solution)/shard_map/dynamic_slice | solution.py:340
  26.9 1.2 %dynamic_slice.7 = s32[1]{0:T(128)} dynamic-slice(s32[64]{0:T(128)} %param.11, s32[]{:T(128)S(6)} %select_n.111), dynamic_slice_sizes={1} | dynamic-slice | bytes 12 | tf_op jit(solution)/shard_map/dynamic_slice | solution.py:341
  28.8 0.7 iota_compare_fusion.3
  29.5 1.3 %pad_add_fusion.info = s32[2]{0:T(128)} fusion(s32[1]{0:T(128)} %dynamic_slice.7, s32[1]{0:T(128)} %bitcast), kind=kLoop, calls=%fused_computation.44 | loop fusion | flops 2 | bytes 16 | tf_op jit(solution)/shard_map/stack | solution.py:354
  30.8 1.3 %reshape.315.gin_ref = f32[1,384]{1,0:T(1,128)} reshape(f32[384]{0:T(512)} %param.17) | data formatting | bytes 3072 | tf_op jit(solution)/shard_map/reshape | solution.py:357
  32.1 0.1 broadcast_and_fusion
  32.2 0.1 add_multiply_fusion
  32.2 0.4 fusion.5
  32.7 0.3 fusion.6
  33.0 0.1 reshape.318
  33.0 0.1 and.138
  33.1 0.1 and.139
  33.2 0.8 pad.37
  34.1 0.1 div.34
  34.2 0.1 rem.77
  34.3 1.0 %reshape.311 = bf16[6,3,1728]{2,1,0:T(4,128)(2,1)S(1)} reshape(bf16[6,27,192]{2,1,0:T(8,128)(2,1)} %param.15) | data formatting | bytes 124416 | tf_op jit(solution)/shard_map/reshape | solution.py:302
  35.4 0.7 pad_maximum_fusion.x_ref
  36.1 45.9 %gather.19 = bf16[2,64,8,3840]{3,2,1,0:T(8,128)(2,1)} custom-call(bf16[2,8,3840]{2,1,0:T(8,128)(2,1)} %pad_maximum_fusion.x_ref), custom_call_target="tpu_custom_call" | custom-call | tf_op jit(solution)/shard_map/gather/pallas_call | solution.py:286
  81.9 0.0 copy-done.1
  81.9 0.6 pad_bitcast_fusion.gout_ref
  82.5 0.0 all-to-all-done
  82.6 0.2 reduce.1
  82.7 0.2 reshape.309
  83.0 1.4 %gather_fusion.2 = bf16[384,16]{1,0:T(8,128)(2,1)S(1)} fusion(bf16[1024,16]{1,0:T(8,128)(2,1)S(1)} %reshape.309, s32[1024]{0:T(1024)S(1)} %pad_clamp_fusion), kind=kCustom, calls=%fused_computation.2 | custom fusion | bytes 26112 | tf_op jit(solution)/shard_map/gather | solution.py:351
  84.4 0.1 copy.21
  84.5 0.7 pad.35.xt_ref
  85.2 11.1 %decode.1 = bf16[1,4,8,6144]{3,2,1,0:T(8,128)(2,1)} custom-call(s32[2]{0:T(128)} %pad_add_fusion.info, bf16[16,768]{1,0:T(8,128)(2,1)} %pad.35.xt_ref, bf16[432,384]{1,0:T(8,128)(2,1)} %bitcast.27, bf16[2,512,3840]{2,1,0:T(8,128)(2,1)} %bitcast.25, f32[1,384]{1,0:T(1,128)} %reshape.315.gin_ref, f32[1,192]{1,0:T(1,128)} %bitcast.29, ...), custom_call_target="tpu_custom_call" | custom-call | tf_op jit(solution)/shard_map/decode/pallas_call | solution.py:178
  (22 shorter events, 0.3 us)
Async XLA Ops:
  0.0 3.8 %copy-start = (bf16[1,16384]{1,0:T(2,128)(2,1)S(1)}, bf16[1,16384]{1,0:T(2,128)(2,1)}, u32[]{:S(2)}) copy-start(bf16[1,16384]{1,0:T(2,128)(2,1)} %param.10) | copy-start | bytes 98308
  0.0 81.9 %copy-start.1 = (f32[96]{0:T(128)S(1)}, f32[96]{0:T(128)}, u32[]{:S(2)}) copy-start(f32[96]{0:T(128)} %param.19) | copy-start | bytes 1156
  6.6 75.9 %all-to-all-start = ((bf16[64,2,128]{2,1,0:T(2,128)(2,1)}), bf16[64,2,128]{2,1,0:T(2,128)(2,1)S(1)}, u32[]{:S(2)}, u32[]{:S(2)}) async-start(bf16[64,2,128]{2,1,0:T(2,128)(2,1)} %reshape.348), calls=%async_computation | async-start | bytes 65536 | tf_op jit(solution)/shard_map/all_to_all | solution.py:337

commit v3 on v2

--- a/solution.py
+++ b/solution.py
@@ -14,7 +14,8 @@
 C1P = 512
 NB = 1792
 MIDH = 3 * NB // 2
-HALF = MIDH + 9 * 128
+HALF = MIDH
+OB = 896
 MID_PARTS = (
     (0, 0, 0, 0, NB),
     (1, 0, NB, 0, NB // 2),
@@ -115,15 +116,28 @@
 
     src = iota((C2, 512), 0)
     dst = iota((C2, 512), 1)
-    low = ((dst // 8 * 3 + dst % 8 == src) & (dst % 8 < 3)).astype(F32).astype(BF16)
-    high = ((dst // 8 * 3 + dst % 8 - 4 == src) & (dst % 8 >= 4) & (dst % 8 < 7)).astype(F32)
-    high = high.astype(BF16)
-    both = jnp.dot(act2[0:768, :], low, preferred_element_type=F32)
-    both += jnp.dot(act2[192:960, :], high, preferred_element_type=F32)
-    lhs[0] = both.astype(BF16)
-    lhs[1] = jnp.dot(act2[384:1152, :], low, preferred_element_type=F32).astype(BF16)
-    z2[...] = jnp.dot(lhs[0], w_ref[0, :, MIDH:HALF], preferred_element_type=F32)
-    z2[...] += jnp.dot(lhs[1], w_ref[1, :, MIDH:HALF], preferred_element_type=F32)
+
+    def place_out(pairs):
+        hit = jnp.zeros((C2, 512), F32)
+        for i, r in pairs:
+            hit += ((dst % 8 == r) & (dst // 8 * 3 + i == src)).astype(F32)
+        return hit.astype(BF16)
+
+    first = place_out(((2, 6),))
+    lhs[0] = jnp.dot(act2[...], place_out(((0, 6), (1, 7))), preferred_element_type=F32).astype(BF16)
+    mixed = jnp.dot(act2[0:768, :], first, preferred_element_type=F32)
+    mixed += jnp.dot(act2[192:960, :], place_out(((2, 7),)), preferred_element_type=F32)
+    lhs[1, 0:768] = mixed.astype(BF16)
+    z2[...] = jnp.dot(lhs[1, 0:768], w_ref[1, :, 0:OB], preferred_element_type=F32)
+    last = jnp.dot(act2[384:1152, :], first, preferred_element_type=F32)
+    lhs[1, 0:768] = last.astype(BF16)
+    z2[...] += jnp.dot(lhs[1, 0:768], w_ref[1, :, OB : 2 * OB], preferred_element_type=F32)
+    for a in range(3):
+        z2[...] += jnp.dot(
+            lhs[0, 192 * a : 192 * a + 768],
+            w_ref[0, :, OB * a : OB * a + OB],
+            preferred_element_type=F32,
+        )
 
     xpos = iota((96, 1), 0) % WL
     gout = gout_ref[...]
@@ -134,7 +148,12 @@
             z = []
             for e in range(3):
                 k = 3 * b + e
-                block = z2[192 * t : 192 * t + 192, 128 * k : 128 * k + 128].reshape(6, 2, 16, 128)
+                at, off = C3 * k // 128 * 128, C3 * k % 128
+                wide = 128 if off + C3 <= 128 else 256
+                block = z2[192 * t : 192 * t + 192, at : at + wide]
+                if off:
+                    block = pltpu.roll(block, wide - off, 1)
+                block = block[:, :128].reshape(6, 2, 16, 128)
                 z.append((block[:, 0].reshape(96, 128), block[:, 1].reshape(96, 128)))
             left = (jnp.where(xpos == 0, 0.0, pltpu.roll(z[0][1], 1, 0)), z[0][0])
             right = (z[2][1], jnp.where(xpos == WL - 1, 0.0, pltpu.roll(z[2][0], 95, 0)))
@@ -153,6 +172,7 @@
                         h = c[0][16:80] + c[1][16:80] + c[2][32:96]
                     else:
                         h = c[0][0:64] + c[1][16:80] + c[2][16:80]
+                    h = jnp.where(lanes < C3, h, 0.0)
                     phases.append(jnp.where(t < count, silu_norm(h, gout, C3), 0.0))
             r1 = pltpu.roll(phases[1], 96, 1)
             r2 = pltpu.roll(phases[2], 64, 1)
@@ -186,15 +206,17 @@
             pltpu.VMEM((384, C1P), BF16),
             pltpu.VMEM((256, NB), F32),
             pltpu.VMEM((1152, C2), BF16),
-            pltpu.VMEM((2, 768, 512), BF16),
-            pltpu.VMEM((768, 1152), F32),
+            pltpu.VMEM((2, 1152, 512), BF16),
+            pltpu.VMEM((768, OB), F32),
             pltpu.VMEM((3, 512, 128), F32),
         ],
         compiler_params=pltpu.CompilerParams(vmem_limit_bytes=56 * 1024 * 1024),
     )(info, xt, win, weights, gin, gmid, gout)
 
 
-def gather_kernel(x_ref, g_ref, own_sem, send_sem, recv_sem):
+def gather_kernel(
+    x_ref, o_ref, g_ref, t_ref, m_ref, own_sem, send_sem, recv_sem, tok_local, tok_send, tok_recv
+):
     grp = lax.axis_index("grp")
     row = lax.axis_index("row")
     core = row % 2
@@ -210,10 +232,13 @@
     right2, left2 = (slot(i1, i2 + 1), row), (slot(i1, i2 + 7), row)
     partner = (grp, row + 1 - 2 * core)
 
+    y, z = grp % 8, grp // 8
     barrier = pltpu.get_barrier_semaphore()
-    for peer in (right1, left1, right2, left2, partner):
-        pl.semaphore_signal(barrier, inc=1, device_id=peer, device_id_type=MESH)
-    pl.semaphore_wait(barrier, 5)
+    pl.semaphore_signal(barrier, inc=1, device_id=partner, device_id_type=MESH)
+    for d in range(1, 8):
+        for peer in (z * 8 + (y + d) % 8, (z + d) % 8 * 8 + y):
+            pl.semaphore_signal(barrier, inc=1, device_id=(peer, row), device_id_type=MESH)
+    pl.semaphore_wait(barrier, 15)
 
     started = []
 
@@ -250,6 +275,31 @@
     for copy in local:
         copy.start()
 
+    def tokens_y(d):
+        return pltpu.make_async_remote_copy(
+            src_ref=o_ref.at[:, (y + d) % 8],
+            dst_ref=m_ref.at[y],
+            send_sem=tok_send.at[0, d],
+            recv_sem=tok_recv.at[0, d],
+            device_id=(z * 8 + (y + d) % 8, row),
+            device_id_type=MESH,
+        )
+
+    def tokens_z(d):
+        return pltpu.make_async_remote_copy(
+            src_ref=m_ref.at[:, (z + d) % 8],
+            dst_ref=t_ref.at[z],
+            send_sem=tok_send.at[1, d],
+            recv_sem=tok_recv.at[1, d],
+            device_id=((z + d) % 8 * 8 + y, row),
+            device_id_type=MESH,
+        )
+
+    tok_own = pltpu.make_async_copy(o_ref.at[:, y], m_ref.at[y], tok_local.at[0])
+    tok_own.start()
+    for d in range(1, 8):
+        tokens_y(d).start()
+
     line = [0, -1, 1, -2, 2, -3, 3, -4]
     for off in line[1:]:
         arrived(core, slot(i1 + off + 8, i2))
@@ -260,6 +310,14 @@
         send(2, right2, i1 + off + 8, i2)
         send(3, left2, i1 + off + 8, i2)
         send(4, partner, i1 + off + 8, i2)
+
+    tok_own.wait()
+    for d in range(1, 8):
+        tokens_y(d).wait()
+    tok_own = pltpu.make_async_copy(m_ref.at[:, z], t_ref.at[z], tok_local.at[1])
+    tok_own.start()
+    for d in range(1, 8):
+        tokens_z(d).start()
 
     for dist in range(1, 5):
         for n, off in enumerate(line):
@@ -279,34 +337,41 @@
         copy.wait_send()
     for copy in local:
         copy.wait()
-
-
-def gather_weights(x):
+    tok_own.wait()
+    for d in range(1, 8):
+        tokens_z(d).wait()
+
+
+def exchange(x, outgoing):
     any_spec = pl.BlockSpec(memory_space=pl.ANY)
+    block = jax.ShapeDtypeStruct((8, 8, 2, 128), BF16)
     return pl.pallas_call(
         gather_kernel,
-        name="gather",
-        out_shape=jax.ShapeDtypeStruct((2, 64, 8, HALF), BF16),
-        in_specs=[any_spec],
-        out_specs=any_spec,
+        name="exchange",
+        out_shape=(jax.ShapeDtypeStruct((2, 64, 8, HALF), BF16), block, block),
+        in_specs=[any_spec] * 2,
+        out_specs=(any_spec,) * 3,
         scratch_shapes=[
             pltpu.SemaphoreType.DMA((2,)),
             pltpu.SemaphoreType.DMA((5, 64)),
             pltpu.SemaphoreType.DMA((2, 64)),
+            pltpu.SemaphoreType.DMA((2,)),
+            pltpu.SemaphoreType.DMA((2, 8)),
+            pltpu.SemaphoreType.DMA((2, 8)),
         ],
         compiler_params=pltpu.CompilerParams(collective_id=0, has_side_effects=True),
-    )(x)
+    )(x, outgoing)
 
 
 def pack_weights(w_mid, w_out):
-    mid = w_mid.reshape(6, 3, 9 * C2)
-    mid = jnp.pad(mid, ((0, 2), (0, 0), (0, NB - 9 * C2))).reshape(8, 3 * NB)
-    out = jnp.pad(w_out, ((0, 0), (0, 0), (0, 128 - C3))).reshape(3, 3, 9 * 128)
-    out = jnp.pad(out.transpose(1, 0, 2), ((0, 1), (0, 1), (0, 0))).reshape(2, 8, 9 * 128)
-    halves = [
-        jnp.concatenate([mid[:, h * MIDH : (h + 1) * MIDH], out[h]], axis=1) for h in range(2)
-    ]
-    return jnp.stack(halves)
+    mid = jnp.pad(w_mid.reshape(6, 3, 9 * C2), ((0, 0), (0, 0), (0, NB - 9 * C2)))
+    out = jnp.pad(w_out.reshape(3, 3, 9 * C3), ((0, 0), (0, 0), (0, OB - 9 * C3)))
+    none = jnp.zeros((OB,), BF16)
+    extra = [out[0, 0], out[0, 1], out[0, 2], out[2, 0], out[2, 2], none]
+    extra += [out[1, 0], out[1, 1], out[1, 2], out[2, 1], none, none]
+    extra = jnp.concatenate(extra).reshape(2, 3 * NB)
+    piece = jnp.concatenate([mid.reshape(6, 3 * NB), extra], axis=0)
+    return jnp.stack([piece[:, :HALF], piece[:, HALF:]])
 
 
 def per_device(latents, frames, offsets, assign, w_in, w_mid, w_out, gain_in, gain_mid, gain_out):
@@ -318,7 +383,6 @@
     cap_tokens = cap_vals // channels
     span_len = cap_tokens // FMAX
 
-    weights = gather_weights(pack_weights(w_mid, w_out)).reshape(2, 8 * groups, HALF)
     win = w_in.transpose(1, 0, 2).reshape(27 * channels, C1)
 
     table = latents.reshape(128, 128)
@@ -334,11 +398,12 @@
         rows = jnp.where((shift & bit) != 0, moved, rows)
     keep = jnp.arange(cap_vals, dtype=jnp.int32)[None, :] < length[:, None]
     outgoing = jnp.where(keep, rows[:, :cap_vals], jnp.zeros((), BF16))
-    incoming = lax.all_to_all(outgoing, "grp", split_axis=0, concat_axis=0, tiled=True)
+    weights, incoming, _ = exchange(pack_weights(w_mid, w_out), outgoing.reshape(8, 8, 2, 128))
+    weights = weights.reshape(2, 8 * groups, HALF)
 
     tokens = incoming.reshape(groups * cap_tokens, channels)
-    request = assign[group_index]
-    count = frames[request]
+    mine = jnp.arange(groups, dtype=jnp.int32) == group_index
+    count = jnp.sum(jnp.where(mine, frames[assign], 0))
     fill_len = count * span_len
     frame_ids = jnp.arange(FMAX, dtype=jnp.int32)[:, None, None]
     row_ids = row_index * RL - 2 + jnp.arange(6, dtype=jnp.int32)[None, :, None]

time: 96.7 us -> 85.2 us (0.88)
  starting transfers between devices: 17.1 us -> 0 us
  Pallas kernels: 57 us -> 63.8 us
  between operations: 2.86 us -> 0.85 us
  local copies, waits for them, and re-layouts: 13.5 us -> 14.5 us
    all_to_all x1 -> x0, starting transfers between devices: 17.1 us -> none  [per_device(): lax.all_to_all(outgoing, 'grp', split_axis=0, concat_axis=0, tiled=True)]
    pallas_call x1, Pallas kernels: 45.9 us -> 50 us  [exchange(): pl.pallas_call(gather_kernel, name='exchange', out_shape=(jax.ShapeDtypeS...]
    pallas_call x1, Pallas kernels: 11.1 us -> 13.8 us  [decode(): pl.pallas_call(decode_kernel, name='decode', out_shape=jax.ShapeDtypeStru...]
    dynamic_slice x2 -> x0, local copies, waits for them, and re-layouts: 2.48 us -> none  [the longest x1 1.24 us: per_device(): request = assign[group_index]]
    unnamed x6 -> x14, local copies, waits for them, and re-layouts: 0.64 us -> 2.12 us
    reshape x4, local copies, waits for them, and re-layouts: 1.09 us -> 2.52 us  [the longest x1 1.03 us: pack_weights(): w_mid.reshape(6, 3, 9 * C2)]
  transfers between devices with their start and end apart: 1 -> 0, of which waited for: 0 -> 0; matrix products, arithmetic and copies ran while one was open for 11% -> 0% of each run, Pallas kernels for 48% -> 0%
where the time goes in v3:
time: 85.2 us; the launch traced here: 84.8 us
  Pallas kernels  63.8 us (75%)
  local copies, waits for them, and re-layouts  14.5 us (17%)
  other arithmetic  5.39 us (6%)
    pallas_call x1, Pallas kernels, exchange(): pl.pallas_call(gather_kernel, name='exchange', out_shape=(jax.ShapeDtypeS...  50 us
    pallas_call x1, Pallas kernels, decode(): pl.pallas_call(decode_kernel, name='decode', out_shape=jax.ShapeDtypeStru...  13.8 us
    unnamed x14, local copies, waits for them, and re-layouts  2.12 us

profile of v3, /device:TPU:1, one launch (start us, length us, event | category | flops | bytes accessed | tf_op | source)
XLA Modules:
  0.0 84.8 jit_solution(2591125036440509198)
XLA Ops:
  0.0 0.7 compare_select_fusion.1
  0.7 1.2 %pad_bitcast_fusion.1.gout_ref = f32[1,128]{1,0:T(1,128)} fusion(f32[96]{0:T(128)} %param.19), kind=kLoop, calls=%fused_computation.57 | loop fusion | bytes 896 | tf_op jit(solution)/shard_map/reshape | solution.py:420
  2.0 0.1 add_multiply_fusion
  2.0 1.2 %reshape.315.gin_ref = f32[1,384]{1,0:T(1,128)} reshape(f32[384]{0:T(512)} %param.17) | data formatting | bytes 3072 | tf_op jit(solution)/shard_map/reshape | solution.py:422
  3.3 1.4 %gather_fusion.1 = s32[64]{0:T(128)S(1)} fusion(s32[64]{0:T(128)} %param.12, s32[1024]{0:T(1024)S(1)} %pad_clamp_fusion.1), kind=kCustom, calls=%fused_computation.1 | custom fusion | bytes 768 | tf_op jit(solution)/shard_map/gather | solution.py:389
  4.7 1.4 %gather_fusion = s32[64]{0:T(128)S(1)} fusion(s32[64]{0:T(128)} %param.11, s32[1024]{0:T(1024)S(1)} %pad_clamp_fusion.1), kind=kCustom, calls=%fused_computation | custom fusion | bytes 768 | tf_op jit(solution)/shard_map/gather | solution.py:406
  6.2 0.6 broadcast_multiply_fusion
  7.5 1.2 %pad_add_fusion.info = s32[2]{0:T(128)} fusion(s32[1]{0:T(128)} %bitcast.1, s32[1]{0:T(128)} %bitcast), kind=kLoop, calls=%fused_computation.56 | loop fusion | flops 2 | bytes 16 | tf_op jit(solution)/shard_map/stack | solution.py:419
  8.7 0.6 iota_compare_fusion.3
  9.4 0.1 broadcast_and_fusion
  9.5 0.3 fusion.8
  9.8 0.1 reshape.318
  9.9 0.1 and.138
  9.9 0.1 and.139
  10.0 0.8 %reshape.307 = bf16[3,3,864]{2,1,0:T(4,128)(2,1)S(1)} reshape(bf16[3,27,96]{2,1,0:T(8,128)(2,1)} %param.16) | data formatting | bytes 31104 | tf_op jit(solution)/shard_map/reshape | solution.py:368
  10.9 0.1 slice_reduce_fusion
  11.0 0.2 dynamic-update-slice
  11.2 0.2 dynamic-update-slice.1
  11.4 0.2 dynamic-update-slice.2
  11.6 0.2 dynamic-update-slice.3
  11.8 0.2 dynamic-update-slice.4
  12.0 0.2 dynamic-update-slice.5
  12.2 0.2 dynamic-update-slice.6
  12.4 0.2 dynamic-update-slice.7
  12.6 0.2 dynamic-update-slice.8
  12.8 0.2 dynamic-update-slice.9
  13.1 0.3 dynamic-update-slice.10
  13.3 0.4 fusion.7
  13.8 0.1 div.34
  13.8 0.1 rem.77
  14.0 0.1 add.169
  14.2 0.2 reduce.9
  14.4 0.2 convolution_convert_fusion
  14.6 0.1 slice.68
  14.7 0.1 pad_select_fusion.1
  14.8 0.1 slice.69
  14.9 0.1 pad_select_fusion
  15.0 0.1 slice.70
  15.1 0.1 fusion
  15.2 0.6 reshape.311.o_ref
  15.8 1.0 %reshape.305 = bf16[6,3,1728]{2,1,0:T(4,128)(2,1)S(1)} reshape(bf16[6,27,192]{2,1,0:T(8,128)(2,1)} %param.15) | data formatting | bytes 124416 | tf_op jit(solution)/shard_map/reshape | solution.py:367
  16.9 0.7 pad_maximum_fusion.x_ref
  17.6 50.0 %exchange.1 = (bf16[2,64,8,2688]{3,2,1,0:T(8,128)(2,1)}, bf16[8,8,2,128]{3,2,1,0:T(2,128)(2,1)}, bf16[8,8,2,128]{3,2,1,0:T(2,128)(2,1)}) custom-call(bf16[2,8,2688]{2,1,0:T(8,128)(2,1)} %pad_maximum_fusion.x_ref, bf16[8,8,2,128]{3,2,1,0:T(2,128)(2,1)} %reshape.311.o_ref), custom_call_target="tpu_custom_call" | custom-call | tf_op jit(solution)/shard_map/exchange/pallas_call | solution.py:348
  67.6 1.0 %reshape.312 = bf16[1024,16]{1,0:T(8,128)(2,1)S(1)} reshape(bf16[8,8,2,128]{3,2,1,0:T(2,128)(2,1)} %get-tuple-element.7) | data formatting | bytes 65536 | tf_op jit(solution)/shard_map/reshape | solution.py:404
  68.6 1.6 %gather_fusion.2 = bf16[384,16]{1,0:T(8,128)(2,1)S(1)} fusion(bf16[1024,16]{1,0:T(8,128)(2,1)S(1)} %reshape.312, s32[1024]{0:T(1024)S(1)} %pad_clamp_fusion), kind=kCustom, calls=%fused_computation.2 | custom fusion | bytes 26112 | tf_op jit(solution)/shard_map/gather | solution.py:416
  70.2 0.1 copy.12
  70.3 0.7 pad.33.xt_ref
  71.0 13.8 %decode.1 = bf16[1,4,8,6144]{3,2,1,0:T(8,128)(2,1)} custom-call(s32[2]{0:T(128)} %pad_add_fusion.info, bf16[16,768]{1,0:T(8,128)(2,1)} %pad.33.xt_ref, bf16[432,384]{1,0:T(8,128)(2,1)} %bitcast.23, bf16[2,512,2688]{2,1,0:T(8,128)(2,1)} %bitcast.21, f32[1,384]{1,0:T(1,128)} %reshape.315.gin_ref, f32[1,192]{1,0:T(1,128)} %bitcast.24, ...), custom_call_target="tpu_custom_call" | custom-call | tf_op jit(solution)/shard_map/decode/pallas_call | solution.py:198
  (21 shorter events, 0.4 us)
Async XLA Ops:
  0.0 14.2 %copy-start = (bf16[1,16384]{1,0:T(2,128)(2,1)S(1)}, bf16[1,16384]{1,0:T(2,128)(2,1)}, u32[]{:S(2)}) copy-start(bf16[1,16384]{1,0:T(2,128)(2,1)} %param.10) | copy-start | bytes 98308

commit v4 on v3

--- a/solution.py
+++ b/solution.py
@@ -228,7 +228,6 @@
     def slot(a, b):
         return (a % 8) * step1 + (b % 8) * step2
 
-    right1, left1 = (slot(i1 + 1, i2), row), (slot(i1 + 7, i2), row)
     right2, left2 = (slot(i1, i2 + 1), row), (slot(i1, i2 + 7), row)
     partner = (grp, row + 1 - 2 * core)
 
@@ -242,12 +241,12 @@
 
     started = []
 
-    def send(way, peer, a, b, own=False):
+    def send(way, peer, a, b, own=False, tag=None):
         at = slot(a, b)
         copy = pltpu.make_async_remote_copy(
             src_ref=x_ref.at[core] if own else g_ref.at[core, at],
             dst_ref=g_ref.at[core, at],
-            send_sem=send_sem.at[way, at],
+            send_sem=send_sem.at[way, at if tag is None else tag],
             recv_sem=recv_sem.at[core, at],
             device_id=peer,
             device_id_type=MESH,
@@ -265,10 +264,10 @@
             device_id_type=MESH,
         ).wait_recv()
 
-    send(0, right1, i1, i2, True)
-    send(1, left1, i1, i2, True)
-    send(2, right2, i1, i2, True)
-    send(3, left2, i1, i2, True)
+    for d in (1, 7, 2, 6, 3, 5, 4):
+        send(0, (slot(i1 + d, i2), row), i1, i2, True, tag=d)
+    send(1, right2, i1, i2, True)
+    send(2, left2, i1, i2, True)
     local = [
         pltpu.make_async_copy(x_ref.at[h], g_ref.at[h, grp], own_sem.at[h]) for h in range(2)
     ]
@@ -303,13 +302,9 @@
     line = [0, -1, 1, -2, 2, -3, 3, -4]
     for off in line[1:]:
         arrived(core, slot(i1 + off + 8, i2))
-        if -4 < off < 0:
-            send(0, right1, i1 + off + 8, i2)
-        if 0 < off < 3:
-            send(1, left1, i1 + off + 8, i2)
-        send(2, right2, i1 + off + 8, i2)
-        send(3, left2, i1 + off + 8, i2)
-        send(4, partner, i1 + off + 8, i2)
+        send(1, right2, i1 + off + 8, i2)
+        send(2, left2, i1 + off + 8, i2)
+        send(3, partner, i1 + off + 8, i2)
 
     tok_own.wait()
     for d in range(1, 8):
@@ -328,8 +323,8 @@
                 b = i2 + sign * dist + 8
                 arrived(core, slot(a, b))
                 if dist < 3 or (dist == 3 and (n % 2 == 0) == (sign < 0)):
-                    send(2 if sign < 0 else 3, right2 if sign < 0 else left2, a, b)
-                send(4, partner, a, b)
+                    send(1 if sign < 0 else 2, right2 if sign < 0 else left2, a, b)
+                send(3, partner, a, b)
 
     for n in range(1, 64):
         arrived(1 - core, (grp + n) % 64)
@@ -344,16 +339,17 @@
 
 def exchange(x, outgoing):
     any_spec = pl.BlockSpec(memory_space=pl.ANY)
+    vm_spec = pl.BlockSpec(memory_space=pltpu.VMEM)
     block = jax.ShapeDtypeStruct((8, 8, 2, 128), BF16)
     return pl.pallas_call(
         gather_kernel,
         name="exchange",
         out_shape=(jax.ShapeDtypeStruct((2, 64, 8, HALF), BF16), block, block),
-        in_specs=[any_spec] * 2,
-        out_specs=(any_spec,) * 3,
+        in_specs=[vm_spec, any_spec],
+        out_specs=(vm_spec, any_spec, any_spec),
         scratch_shapes=[
             pltpu.SemaphoreType.DMA((2,)),
-            pltpu.SemaphoreType.DMA((5, 64)),
+            pltpu.SemaphoreType.DMA((4, 64)),
             pltpu.SemaphoreType.DMA((2, 64)),
             pltpu.SemaphoreType.DMA((2,)),
             pltpu.SemaphoreType.DMA((2, 8)),
@@ -386,8 +382,10 @@
     win = w_in.transpose(1, 0, 2).reshape(27 * channels, C1)
 
     table = latents.reshape(128, 128)
-    start = offsets[assign]
-    length = frames[assign] * (span_len * channels)
+    packed = (offsets * 8 + frames).at[assign].get(mode="promise_in_bounds")
+    start = packed // 8
+    lasting = packed % 8
+    length = lasting * (span_len * channels)
     first = start // 8
     want = first[:, None] + jnp.arange(3, dtype=jnp.int32)[None, :]
     pick = (want.reshape(-1)[:, None] == jnp.arange(128, dtype=jnp.int32)[None, :]).astype(BF16)
@@ -403,7 +401,7 @@
 
     tokens = incoming.reshape(groups * cap_tokens, channels)
     mine = jnp.arange(groups, dtype=jnp.int32) == group_index
-    count = jnp.sum(jnp.where(mine, frames[assign], 0))
+    count = jnp.sum(jnp.where(mine, lasting, 0))
     fill_len = count * span_len
     frame_ids = jnp.arange(FMAX, dtype=jnp.int32)[:, None, None]
     row_ids = row_index * RL - 2 + jnp.arange(6, dtype=jnp.int32)[None, :, None]

time: 85.2 us -> 80.5 us (0.945)
  Pallas kernels: 63.8 us -> 60.5 us
  local copies, waits for them, and re-layouts: 14.5 us -> 12.5 us
    pallas_call x1, Pallas kernels: 50 us -> 46.7 us  [exchange(): pl.pallas_call(gather_kernel, name='exchange', out_shape=(jax.ShapeDtypeS...]
    gather x2 -> x1, local copies, waits for them, and re-layouts: 2.86 us -> 0.78 us  [per_device(): packed = (offsets * 8 + frames).at[assign].get(mode='promise_in_bounds')]
where the time goes in v4:
time: 80.5 us; the launch traced here: 80 us
  Pallas kernels  60.5 us (75%)
  local copies, waits for them, and re-layouts  12.5 us (16%)
  other arithmetic  6.05 us (8%)
  between operations  0.84 us (1%)
    pallas_call x1, Pallas kernels, exchange(): pl.pallas_call(gather_kernel, name='exchange', out_shape=(jax.ShapeDtypeS...  46.7 us
    pallas_call x1, Pallas kernels, decode(): pl.pallas_call(decode_kernel, name='decode', out_shape=jax.ShapeDtypeStru...  13.8 us
    unnamed x14, local copies, waits for them, and re-layouts  2.12 us
    gather x2, local copies, waits for them, and re-layouts, per_device(): picked = tokens[(shard * cap_tokens + within).reshape(-1)]  1.7 us

profile of v4, /device:TPU:1, one launch (start us, length us, event | category | flops | bytes accessed | tf_op | source)
XLA Modules:
  0.0 80.0 jit_solution(1425758783650452428)
XLA Ops:
  0.0 0.7 multiply_add_fusion
  0.7 0.7 compare_select_fusion.1
  1.4 1.2 %pad_bitcast_fusion.1.gout_ref = f32[1,128]{1,0:T(1,128)} fusion(f32[96]{0:T(128)} %param.19), kind=kLoop, calls=%fused_computation.61 | loop fusion | bytes 896 | tf_op jit(solution)/shard_map/reshape | solution.py:418
  2.6 0.1 add_multiply_fusion
  2.7 1.2 %reshape.341.gin_ref = f32[1,384]{1,0:T(1,128)} reshape(f32[384]{0:T(512)} %param.17) | data formatting | bytes 3072 | tf_op jit(solution)/shard_map/reshape | solution.py:420
  4.0 0.8 gather_fusion
  4.8 0.6 broadcast_multiply_fusion
  6.1 1.2 %pad_add_fusion.info = s32[2]{0:T(128)} fusion(s32[1]{0:T(128)} %bitcast.1, s32[1]{0:T(128)} %bitcast), kind=kLoop, calls=%fused_computation.60 | loop fusion | flops 2 | bytes 16 | tf_op jit(solution)/shard_map/stack | solution.py:417
  7.3 0.6 iota_compare_fusion.3
  8.0 0.1 broadcast_and_fusion
  8.0 0.3 fusion.8
  8.3 0.1 reshape.344
  8.4 0.1 and.179
  8.5 0.1 and.180
  8.6 0.8 %reshape.333 = bf16[3,3,864]{2,1,0:T(4,128)(2,1)S(1)} reshape(bf16[3,27,96]{2,1,0:T(8,128)(2,1)} %param.16) | data formatting | bytes 31104 | tf_op jit(solution)/shard_map/reshape | solution.py:364
  9.4 0.1 slice_reduce_fusion
  9.6 0.2 dynamic-update-slice
  9.8 0.2 dynamic-update-slice.1
  10.0 0.2 dynamic-update-slice.2
  10.2 0.2 dynamic-update-slice.3
  10.4 0.2 dynamic-update-slice.4
  10.6 0.2 dynamic-update-slice.5
  10.8 0.2 dynamic-update-slice.6
  11.0 0.2 dynamic-update-slice.7
  11.2 0.2 dynamic-update-slice.8
  11.4 0.2 dynamic-update-slice.9
  11.6 0.3 dynamic-update-slice.10
  11.9 0.4 fusion.7
  12.3 0.1 div.45
  12.4 0.1 rem.97
  12.6 0.1 add.194
  12.8 0.2 reduce.9
  13.0 0.2 convolution_convert_fusion
  13.2 0.1 slice.66
  13.3 0.1 pad_select_fusion.1
  13.4 0.1 slice.67
  13.5 0.1 pad_select_fusion
  13.6 0.1 slice.68
  13.6 0.1 fusion
  13.7 0.6 reshape.337.o_ref
  14.4 1.0 %reshape.331 = bf16[6,3,1728]{2,1,0:T(4,128)(2,1)S(1)} reshape(bf16[6,27,192]{2,1,0:T(8,128)(2,1)} %param.15) | data formatting | bytes 124416 | tf_op jit(solution)/shard_map/reshape | solution.py:363
  15.5 0.7 pad_maximum_fusion.x_ref
  16.2 46.7 %exchange.1 = (bf16[2,64,8,2688]{3,2,1,0:T(8,128)(2,1)}, bf16[8,8,2,128]{3,2,1,0:T(2,128)(2,1)}, bf16[8,8,2,128]{3,2,1,0:T(2,128)(2,1)}) custom-call(bf16[2,8,2688]{2,1,0:T(8,128)(2,1)} %pad_maximum_fusion.x_ref, bf16[8,8,2,128]{3,2,1,0:T(2,128)(2,1)} %reshape.337.o_ref), custom_call_target="tpu_custom_call" | custom-call | tf_op jit(solution)/shard_map/exchange/pallas_call | solution.py:344
  62.8 1.0 %reshape.338 = bf16[1024,16]{1,0:T(8,128)(2,1)S(1)} reshape(bf16[8,8,2,128]{3,2,1,0:T(2,128)(2,1)} %get-tuple-element.7) | data formatting | bytes 65536 | tf_op jit(solution)/shard_map/reshape | solution.py:402
  63.8 1.6 %gather_fusion.1 = bf16[384,16]{1,0:T(8,128)(2,1)S(1)} fusion(bf16[1024,16]{1,0:T(8,128)(2,1)S(1)} %reshape.338, s32[1024]{0:T(1024)S(1)} %pad_clamp_fusion), kind=kCustom, calls=%fused_computation.1 | custom fusion | bytes 26112 | tf_op jit(solution)/shard_map/gather | solution.py:414
  65.4 0.1 copy.12
  65.5 0.7 pad.33.xt_ref
  66.2 13.8 %decode.1 = bf16[1,4,8,6144]{3,2,1,0:T(8,128)(2,1)} custom-call(s32[2]{0:T(128)} %pad_add_fusion.info, bf16[16,768]{1,0:T(8,128)(2,1)} %pad.33.xt_ref, bf16[432,384]{1,0:T(8,128)(2,1)} %bitcast.23, bf16[2,512,2688]{2,1,0:T(8,128)(2,1)} %bitcast.21, f32[1,384]{1,0:T(1,128)} %reshape.341.gin_ref, f32[1,192]{1,0:T(1,128)} %bitcast.24, ...), custom_call_target="tpu_custom_call" | custom-call | tf_op jit(solution)/shard_map/decode/pallas_call | solution.py:198
  (20 shorter events, 0.3 us)
Async XLA Ops:
  0.0 12.8 %copy-start = (bf16[1,16384]{1,0:T(2,128)(2,1)S(1)}, bf16[1,16384]{1,0:T(2,128)(2,1)}, u32[]{:S(2)}) copy-start(bf16[1,16384]{1,0:T(2,128)(2,1)} %param.10) | copy-start | bytes 98308

commit v5 on v4

--- a/solution.py
+++ b/solution.py
@@ -63,7 +63,7 @@
     h = lax.dot_general(
         cols[...], win_ref[...], (((0,), (0,)), ((), ())), preferred_element_type=F32
     )
-    act = silu_norm(h, gin_ref[...], C1).astype(BF16)
+    act = silu_norm(h, gin_ref[...].reshape(1, -1), C1).astype(BF16)
     src = iota((C1, C1P), 0)
     dst = iota((C1, C1P), 1)
     place = ((dst // 8 * 6 + dst % 8 == src) & (dst % 8 < 6)).astype(F32).astype(BF16)
@@ -88,7 +88,7 @@
 
     act2[0:384, :] = jnp.zeros((384, C2), BF16)
     xpos = iota((64, 1), 0) % WL
-    gmid = gmid_ref[...]
+    gmid = gmid_ref[...].reshape(1, -1)
     for t in range(FMAX):
         combos = []
         for b in range(3):
@@ -306,15 +306,15 @@
         send(2, left2, i1 + off + 8, i2)
         send(3, partner, i1 + off + 8, i2)
 
-    tok_own.wait()
-    for d in range(1, 8):
-        tokens_y(d).wait()
-    tok_own = pltpu.make_async_copy(m_ref.at[:, z], t_ref.at[z], tok_local.at[1])
-    tok_own.start()
-    for d in range(1, 8):
-        tokens_z(d).start()
-
     for dist in range(1, 5):
+        if dist == 2:
+            tok_own.wait()
+            for d in range(1, 8):
+                tokens_y(d).wait()
+            tok_own = pltpu.make_async_copy(m_ref.at[:, z], t_ref.at[z], tok_local.at[1])
+            tok_own.start()
+            for d in range(1, 8):
+                tokens_z(d).start()
         for n, off in enumerate(line):
             a = i1 + off + 8
             for sign in (-1, 1):
@@ -417,7 +417,7 @@
     info = jnp.stack([row_index.astype(jnp.int32), count])
     gout = jnp.pad(gain_out, (0, 128 - C3)).reshape(1, 128)
     return decode(
-        info, xt, win, weights, gain_in.reshape(1, C1), gain_mid.reshape(1, C2), gout
+        info, xt, win, weights, gain_in, gain_mid, gout
     )
 
 

time: 80.5 us -> 79.2 us (0.984)
  local copies, waits for them, and re-layouts: 12.5 us -> 11.1 us
    reshape x1 -> x0, local copies, waits for them, and re-layouts: 1.25 us -> none  [per_device(): gain_in.reshape(1, C1)]
where the time goes in v5:
time: 79.2 us; the launch traced here: 78.8 us
  Pallas kernels  60.6 us (77%)
  local copies, waits for them, and re-layouts  11.1 us (14%)
  other arithmetic  6.1 us (8%)
  between operations  0.84 us (1%)
    pallas_call x1, Pallas kernels, exchange(): pl.pallas_call(gather_kernel, name='exchange', out_shape=(jax.ShapeDtypeS...  46.7 us
    pallas_call x1, Pallas kernels, decode(): pl.pallas_call(decode_kernel, name='decode', out_shape=jax.ShapeDtypeStru...  13.8 us
    unnamed x14, local copies, waits for them, and re-layouts  2.12 us
    gather x2, local copies, waits for them, and re-layouts, per_device(): picked = tokens[(shard * cap_tokens + within).reshape(-1)]  1.7 us

profile of v5, /device:TPU:1, one launch (start us, length us, event | category | flops | bytes accessed | tf_op | source)
XLA Modules:
  0.0 78.8 jit_solution(11753164236708374386)
XLA Ops:
  0.0 0.7 multiply_add_fusion
  0.7 0.7 compare_select_fusion.1
  1.4 1.2 %pad_bitcast_fusion.1.gout_ref = f32[1,128]{1,0:T(1,128)} fusion(f32[96]{0:T(128)} %param.19), kind=kLoop, calls=%fused_computation.61 | loop fusion | bytes 896 | tf_op jit(solution)/shard_map/reshape | solution.py:418
  2.6 0.1 add_multiply_fusion
  2.6 0.8 gather_fusion
  3.4 0.6 broadcast_multiply_fusion
  4.7 1.3 %pad_add_fusion.info = s32[2]{0:T(128)} fusion(s32[1]{0:T(128)} %bitcast.1, s32[1]{0:T(128)} %bitcast), kind=kLoop, calls=%fused_computation.60 | loop fusion | flops 2 | bytes 16 | tf_op jit(solution)/shard_map/stack | solution.py:417
  6.0 0.6 iota_compare_fusion.3
  6.7 0.1 broadcast_and_fusion
  6.8 0.3 fusion.8
  7.1 0.1 reshape.336
  7.2 0.1 and.179
  7.2 0.1 and.180
  7.3 0.8 %reshape.327 = bf16[3,3,864]{2,1,0:T(4,128)(2,1)S(1)} reshape(bf16[3,27,96]{2,1,0:T(8,128)(2,1)} %param.16) | data formatting | bytes 31104 | tf_op jit(solution)/shard_map/reshape | solution.py:364
  8.2 0.1 slice_reduce_fusion
  8.3 0.2 dynamic-update-slice
  8.5 0.2 dynamic-update-slice.1
  8.7 0.2 dynamic-update-slice.2
  8.9 0.2 dynamic-update-slice.3
  9.1 0.2 dynamic-update-slice.4
  9.3 0.2 dynamic-update-slice.5
  9.5 0.2 dynamic-update-slice.6
  9.7 0.2 dynamic-update-slice.7
  9.9 0.2 dynamic-update-slice.8
  10.1 0.2 dynamic-update-slice.9
  10.4 0.3 dynamic-update-slice.10
  10.6 0.4 fusion.7
  11.1 0.1 div.45
  11.2 0.1 rem.97
  11.3 0.1 iota_add_fusion
  11.3 0.1 add.194
  11.5 0.2 reduce.9
  11.7 0.2 convolution_convert_fusion
  11.9 0.1 slice.66
  12.0 0.1 pad_select_fusion.1
  12.1 0.1 slice.67
  12.2 0.1 pad_select_fusion
  12.3 0.1 slice.68
  12.4 0.1 fusion
  12.5 0.6 reshape.331.o_ref
  13.1 1.0 %reshape.325 = bf16[6,3,1728]{2,1,0:T(4,128)(2,1)S(1)} reshape(bf16[6,27,192]{2,1,0:T(8,128)(2,1)} %param.15) | data formatting | bytes 124416 | tf_op jit(solution)/shard_map/reshape | solution.py:363
  14.2 0.7 pad_maximum_fusion.x_ref
  14.9 46.7 %exchange.1 = (bf16[2,64,8,2688]{3,2,1,0:T(8,128)(2,1)}, bf16[8,8,2,128]{3,2,1,0:T(2,128)(2,1)}, bf16[8,8,2,128]{3,2,1,0:T(2,128)(2,1)}) custom-call(bf16[2,8,2688]{2,1,0:T(8,128)(2,1)} %pad_maximum_fusion.x_ref, bf16[8,8,2,128]{3,2,1,0:T(2,128)(2,1)} %reshape.331.o_ref), custom_call_target="tpu_custom_call" | custom-call | tf_op jit(solution)/shard_map/exchange/pallas_call | solution.py:344
  61.6 1.0 %reshape.332 = bf16[1024,16]{1,0:T(8,128)(2,1)S(1)} reshape(bf16[8,8,2,128]{3,2,1,0:T(2,128)(2,1)} %get-tuple-element.7) | data formatting | bytes 65536 | tf_op jit(solution)/shard_map/reshape | solution.py:402
  62.6 1.6 %gather_fusion.1 = bf16[384,16]{1,0:T(8,128)(2,1)S(1)} fusion(bf16[1024,16]{1,0:T(8,128)(2,1)S(1)} %reshape.332, s32[1024]{0:T(1024)S(1)} %pad_clamp_fusion), kind=kCustom, calls=%fused_computation.1 | custom fusion | bytes 26112 | tf_op jit(solution)/shard_map/gather | solution.py:414
  64.2 0.1 copy.12
  64.3 0.7 pad.33.xt_ref
  65.0 13.8 %decode.1 = bf16[1,4,8,6144]{3,2,1,0:T(8,128)(2,1)} custom-call(s32[2]{0:T(128)} %pad_add_fusion.info, bf16[16,768]{1,0:T(8,128)(2,1)} %pad.33.xt_ref, bf16[432,384]{1,0:T(8,128)(2,1)} %bitcast.22, bf16[2,512,2688]{2,1,0:T(8,128)(2,1)} %bitcast.20, f32[384]{0:T(512)} %gin_ref.1, f32[192]{0:T(256)} %gmid_ref.1, f32[1,128]{1,0:T(1,128)} %pad_bitcast_fusion.1.gout_ref), custom_call_target="tpu_custom_call" | custom-call | tf_op jit(solution)/shard_map/decode/pallas_call | solution.py:198
  (19 shorter events, 0.3 us)
Async XLA Ops:
  0.0 11.5 %copy-start = (bf16[1,16384]{1,0:T(2,128)(2,1)S(1)}, bf16[1,16384]{1,0:T(2,128)(2,1)}, u32[]{:S(2)}) copy-start(bf16[1,16384]{1,0:T(2,128)(2,1)} %param.10) | copy-start | bytes 98308
